TPU v7x, 512 devices: a whole 4x8x8 slice. The times are simulated.
512 devices in a mesh: beam: 16 (over z, x_hi), tile: 32 (over y, x_lo, core).
Axes of the slice: x: 4 (x_hi: 2, x_lo: 2; x = x_hi * 2 + x_lo), y: 8, z: 8, core: 2. Of those that a mesh axis runs over, the one named last changes fastest.
Arguments:
- scattering: float32 [64, 2, 4096, 256], P('beam', None, 'tile'), may hold values from -4 to 4
- potential: float32 [4096, 256], P('tile'), may hold values from -6 to 6
- row_offset: int32 [16, 32], P(None, 'tile'), may hold values from 0 to 64
- col_offset: int32 [16, 32], P(None, 'tile'), may hold values from 0 to 128
- table_index: int32 [16, 32], P(None, 'tile'), may hold values from 0 to 3
- beam_tilt: int32 [2, 64], P(None, 'beam'), may hold values from -8 to 8
- coef_table: float32 [2, 4, 64], P(None, None, 'beam'), may hold values from -0.75 to 0.75
- measured: float32 [16, 32, 128, 128], P(None, 'tile'), may hold values from 0 to 2
Outputs:
- residual: float32 [16, 32, 128, 128], P('beam', 'tile')
- gradient: float32 [4096, 256], P('tile')
All inputs are finite; a program needn't handle non-finite values.
Results may differ from a plain program's by a relative error of at most 0.0002.
Values sent between devices are 32-bit elements; how exact they have to be, the bound alone decides.
No kernel may reach another device: no remote copies, remote signals or barrier semaphores. Data moves between devices by JAX's collectives and lax.ppermute only.
A program may use at most 64 MiB of HBM per device.

v0:
```python
import math

import jax
import jax.numpy as jnp
from jax import lax
from jax.sharding import PartitionSpec as P

MARGIN = 32


SIGMA_SCALE = 1.0
HIGH = lax.Precision.HIGHEST


def with_halo(cells, sides, width):
    for axis, dim in sides:
        count = lax.axis_size(axis)
        ends = count - 1
        head = lax.slice_in_dim(cells, 0, width, axis=dim)
        tail = lax.slice_in_dim(cells, cells.shape[dim] - width, cells.shape[dim], axis=dim)
        cells = jnp.concatenate(
            [
                lax.ppermute(tail, axis, [(i, (i + 1) % count) for i in range(ends)]),
                cells,
                lax.ppermute(head, axis, [((i + 1) % count, i) for i in range(ends)]),
            ],
            axis=dim,
        )
    return cells


def dft_table(length, inverse):
    pixel_index = jnp.arange(length, dtype=jnp.int32)
    phase_turns = (pixel_index[:, None] * pixel_index[None, :] % length).astype(jnp.float32)
    dft_angle = phase_turns * (2.0 * math.pi / length)
    unit_scale = 1.0 / math.sqrt(length)
    sin_sign = 1.0 if inverse else -1.0
    part_re = jnp.cos(dft_angle) * unit_scale
    part_im = sin_sign * jnp.sin(dft_angle) * unit_scale
    upper = jnp.concatenate([part_re, part_im], 1)
    lower = jnp.concatenate([-part_im, part_re], 1)
    return jnp.concatenate([upper, lower], 0)


def along_last(value_re, value_im, table):
    length = value_re.shape[-1]
    joined = jnp.concatenate([value_re, value_im], -1)
    lead_shape = joined.shape[:-1]
    product = jnp.dot(joined.reshape(-1, 2 * length), table, precision=HIGH)
    product = product.reshape(lead_shape + (2 * length,))
    return (product[..., :length], product[..., length:])


def transform(value_re, value_im, table):
    half_re, half_im = along_last(value_re, value_im, table)
    flip_re = jnp.swapaxes(half_re, -1, -2)
    flip_im = jnp.swapaxes(half_im, -1, -2)
    full_re, full_im = along_last(flip_re, flip_im, table)
    return (jnp.swapaxes(full_re, -1, -2), jnp.swapaxes(full_im, -1, -2))


def finish(summed, start_row, start_col, phase_map, observed, tile_rows, tile_cols):
    patch_len = summed.shape[-1]

    def cut_phase(row_at, col_at):
        return lax.dynamic_slice(phase_map, (row_at, col_at), (patch_len, patch_len))

    local_pot = jax.vmap(cut_phase)(start_row, start_col)
    trans_re = jnp.cos(local_pot)
    trans_im = jnp.sin(local_pot)
    wave_re = summed[:, 0]
    wave_im = summed[:, 1]
    exit_re = trans_re * wave_re - trans_im * wave_im
    exit_im = trans_re * wave_im + trans_im * wave_re
    far_re, far_im = transform(exit_re, exit_im, dft_table(patch_len, False))
    misfit = far_re * far_re + far_im * far_im - observed
    back_re, back_im = transform(misfit * far_re, misfit * far_im, dft_table(patch_len, True))
    pieces = SIGMA_SCALE * (exit_re * back_im - exit_im * back_re)
    offsets = jnp.arange(patch_len, dtype=jnp.int32)
    row_index = start_row[:, None, None] + offsets[None, :, None]
    col_index = start_col[:, None, None] + offsets[None, None, :]
    accum_grid = (
        jnp.zeros((tile_rows + 2 * MARGIN, tile_cols), jnp.float32)
        .at[row_index, col_index]
        .add(pieces)
    )
    return (misfit, accum_grid)


def shards(
    scattering, potential, row_offset, col_offset, table_index, beam_tilt, coef_table, measured
):
    beam_dev = scattering.shape[0]
    tile_rows = scattering.shape[2]
    tile_cols = scattering.shape[3]
    patch_len = measured.shape[-1]
    tile_id = lax.axis_index("tile")
    beam_id = lax.axis_index("beam")
    beam_count = lax.axis_size("beam")
    stacked = jnp.concatenate(
        [scattering.reshape(beam_dev * 2, tile_rows, tile_cols), potential[None]], 0
    )
    extended = with_halo(stacked, (("tile", 1),), MARGIN)
    beam_waves = extended[: 2 * beam_dev].reshape(beam_dev, 2, tile_rows + 2 * MARGIN, tile_cols)
    phase_map = extended[2 * beam_dev] * SIGMA_SCALE
    start_row = row_offset[:, 0]
    start_col = col_offset[:, 0]
    corner_row = start_row + tile_id * tile_rows - MARGIN
    phase_turns = (
        beam_tilt[0][None, :] * corner_row[:, None] + beam_tilt[1][None, :] * start_col[:, None]
    ) % patch_len
    tilt_angle = phase_turns.astype(jnp.float32) * (2.0 * math.pi / patch_len)
    onehot = (
        table_index[:, 0][:, None] == jnp.arange(coef_table.shape[1], dtype=jnp.int32)[None, :]
    ).astype(jnp.float32)
    picked_re = jnp.dot(onehot, coef_table[0], precision=HIGH)
    picked_im = jnp.dot(onehot, coef_table[1], precision=HIGH)
    coef_re = picked_re * jnp.cos(tilt_angle) + picked_im * jnp.sin(tilt_angle)
    coef_im = picked_im * jnp.cos(tilt_angle) - picked_re * jnp.sin(tilt_angle)
    zero_index = jnp.zeros((), jnp.int32)

    def partial_wave(row_at, col_at, weight_re, weight_im):
        region = lax.dynamic_slice(
            beam_waves,
            (zero_index, zero_index, row_at, col_at),
            (beam_dev, 2, patch_len, patch_len),
        )
        wave_re = jnp.einsum("b,bij->ij", weight_re, region[:, 0], precision=HIGH) - jnp.einsum(
            "b,bij->ij", weight_im, region[:, 1], precision=HIGH
        )
        wave_im = jnp.einsum("b,bij->ij", weight_re, region[:, 1], precision=HIGH) + jnp.einsum(
            "b,bij->ij", weight_im, region[:, 0], precision=HIGH
        )
        return jnp.stack([wave_re, wave_im])

    partial_value = jax.vmap(partial_wave)(start_row, start_col, coef_re, coef_im)
    positions = partial_value.shape[0]
    per_beam = positions // beam_count
    first_pos = beam_id * per_beam
    observed_all = measured[:, 0]
    summed = lax.psum_scatter(partial_value, "beam", scatter_dimension=0, tiled=True)
    own_row = lax.dynamic_slice_in_dim(start_row, first_pos, per_beam, 0)
    own_col = lax.dynamic_slice_in_dim(start_col, first_pos, per_beam, 0)
    own_seen = lax.dynamic_slice_in_dim(observed_all, first_pos, per_beam, 0)
    misfit, grad_strip = finish(summed, own_row, own_col, phase_map, own_seen, tile_rows, tile_cols)
    grad_strip = lax.psum(grad_strip, "beam")
    rims = jnp.concatenate([grad_strip[:MARGIN], grad_strip[tile_rows + MARGIN :]], 0)
    beside_all = with_halo(rims, (("tile", 0),), MARGIN)
    core = grad_strip[MARGIN : MARGIN + tile_rows]
    core = core.at[:MARGIN].add(beside_all[:MARGIN])
    core = core.at[tile_rows - MARGIN :].add(beside_all[3 * MARGIN :])
    return (misfit[:, None], core)


def solution(mesh):
    in_specs = (
        P("beam", None, "tile", None),
        P("tile", None),
        P(None, "tile"),
        P(None, "tile"),
        P(None, "tile"),
        P(None, "beam"),
        P(None, None, "beam"),
        P(None, "tile", None, None),
    )
    out_specs = (P("beam", "tile", None, None), P("tile", None))
    return jax.shard_map(shards, mesh=mesh, in_specs=in_specs, out_specs=out_specs, check_vma=False)
```

profile of v0, /device:TPU:27, one launch (start us, length us, event | category | flops | bytes accessed | tf_op | source)
XLA Modules:
  0.0 646.9 jit_solution(3439546859666220270)
XLA Ops:
  11.3 2.4 copy.24
  13.7 2.6 collective-permute-start.1
  17.3 5.1 collective-permute-start
  26.4 2.4 copy.25
  28.7 3.5 pad_maximum_fusion
  32.2 71.0 %while.4 = (s32[]{:T(128)}, f32[4,2,192,256]{2,3,1,0:T(8,128)}, s32[16,4]{0,1:T(4,128)S(1)}, f32[16,4,2,128,128]{4,3,2,1,0:T(8,128)}, s32[]{:T(128)}) while((s32[]{:T(128)}, f32[4,2,192,256]{2,3,1,0:T(8,128)}, s32[16,4]{0,1:T(4,128)S(1)}, f32[16,4,2,128,128]{4,3,2,1,0:T(8,128)}, s32[]{:T(128)}) %tuple.67), condition=%wide.while_cond.3, body=%wide.while_body.3.sunk | while | flops 2 | bytes 3145861 | solution.py:123
  32.8 2.7 constant_dynamic-slice_fusion.8
  37.3 2.7 constant_dynamic-slice_fusion.8
  41.7 2.7 constant_dynamic-slice_fusion.8
  46.1 2.7 constant_dynamic-slice_fusion.8
  50.5 2.7 constant_dynamic-slice_fusion.8
  55.0 2.7 constant_dynamic-slice_fusion.8
  59.4 2.7 constant_dynamic-slice_fusion.8
  63.9 2.7 constant_dynamic-slice_fusion.8
  68.3 2.7 constant_dynamic-slice_fusion.8
  72.7 2.7 constant_dynamic-slice_fusion.8
  77.1 2.7 constant_dynamic-slice_fusion.8
  81.6 2.7 constant_dynamic-slice_fusion.8
  86.1 2.7 constant_dynamic-slice_fusion.8
  90.6 2.7 constant_dynamic-slice_fusion.8
  95.0 2.7 constant_dynamic-slice_fusion.8
  99.4 2.7 constant_dynamic-slice_fusion.8
  103.2 6.4 fusion
  109.6 2.5 copy.45
  112.1 2.5 copy.50
  114.7 2.6 copy.35
  118.5 2.4 add_bitcast_fusion
  134.6 202.8 %reduce-scatter.2.cloned.1.call-done = f32[1,2,128,128]{2,3,1,0:T(8,128)} async-done(((f32[16,2,128,128]{2,3,1,0:T(8,128)}), f32[1,2,128,128]{2,3,1,0:T(8,128)}) %reduce-scatter.2.cloned.1.call-update) | async-done | bytes 131088 | tf_op jit(solution)/shard_map/reduce_scatter | solution.py:141
  343.0 113.6 %scatter_custom_fusion = f32[49152]{0:T(1024)S(1)} fusion(s32[16384]{0:T(1024)} %select_bitcast_fusion, f32[16384]{0:T(1024)S(1)} %bitcast.136, f32[]{:T(128)} %constant.122.clone.1), kind=kCustom, calls=%fused_computation.53 | custom fusion | flops 16384 | bytes 197120
  457.4 155.7 %all-reduce.2.cloned.1.call-done = f32[192,256]{1,0:T(8,128)} async-done(((f32[192,256]{1,0:T(8,128)}), f32[192,256]{1,0:T(8,128)}) %all-reduce.2.cloned.1.call-update) | async-done | bytes 196624 | tf_op jit(solution)/shard_map/psum | solution.py:146
  613.9 17.4 %collective-permute-start.2 = (f32[32,256]{1,0:T(8,128)S(1)}, f32[32,256]{1,0:T(8,128)S(1)}, u32[]{:S(2)}, u32[]{:S(2)}) collective-permute-start(f32[32,256]{1,0:T(8,128)S(1)} %get-tuple-element.88), channel_id=1, source_target_pairs={{0,1},{1,2},{2,3},{3,4},{4,5},{5,6},{6,7},{7,8},{8,9},{9,10},{10,1... | collective-permute-start | bytes 98312 | tf_op jit(solution)/shard_map/ppermute | solution.py:23
  635.7 3.7 collective-permute-done.3
  (149 shorter events, 59.2 us)
Async XLA Ops:
  7.2 119.1 %copy-start = (f32[16,1,128,128]{3,2,1,0:T(8,128)S(1)}, f32[16,1,128,128]{3,2,1,0:T(8,128)}, u32[]{:S(2)}) copy-start(f32[16,1,128,128]{3,2,1,0:T(8,128)} %param.19) | copy-start | bytes 3145732
  7.2 330.2 %reduce-scatter.2.cloned.1.call-start = ((), (), s32[]{:S(2)}) async-start(), calls=%async_computation.1 | async-start | bytes 2228224 | tf_op jit(solution)/shard_map/reduce_scatter | solution.py:141
  11.3 11.1 %copy-start.7 = (s32[2,4]{1,0:T(2,128)S(1)}, s32[2,4]{1,0:T(2,128)}, u32[]{:S(2)}) copy-start(s32[2,4]{1,0:T(2,128)} %param.17) | copy-start | bytes 100
  11.3 11.2 %copy-start.10 = (s32[16,1]{0,1:T(1,128)S(1)}, s32[16,1]{0,1:T(1,128)}, u32[]{:S(2)}) copy-start(s32[16,1]{0,1:T(1,128)} %param.14) | copy-start | bytes 196
  11.3 11.2 %copy-start.11 = (f32[2,4,4]{2,1,0:T(4,128)S(1)}, f32[2,4,4]{2,1,0:T(4,128)}, u32[]{:S(2)}) copy-start(f32[2,4,4]{2,1,0:T(4,128)} %param.18) | copy-start | bytes 388
  11.3 11.2 %copy-start.12 = (s32[16,1]{0,1:T(1,128)S(1)}, s32[16,1]{0,1:T(1,128)}, u32[]{:S(2)}) copy-start(s32[16,1]{0,1:T(1,128)} %param.16) | copy-start | bytes 196
  11.3 11.4 %copy-start.13 = (s32[16,1]{0,1:T(1,128)S(1)}, s32[16,1]{0,1:T(1,128)}, u32[]{:S(2)}) copy-start(s32[16,1]{0,1:T(1,128)} %param.15) | copy-start | bytes 196
  13.7 10.6 %collective-permute-start.1 = (f32[9,32,256]{2,1,0:T(8,128)}, f32[9,32,256]{2,1,0:T(8,128)}, u32[]{:S(2)}, u32[]{:S(2)}) collective-permute-start(f32[9,32,256]{2,1,0:T(8,128)} %copy.24), channel_id=1, source_target_pairs={{1,0},{2,1},{3,2},{4,3},{5,4},{6,5},{7,6},{8,7},{9,8},{10,9},{11,1... | collective-permute-start | bytes 884744 | tf_op jit(solution)/shard_map/ppermute | solution.py:25
  17.3 9.0 %collective-permute-start = (f32[9,32,256]{2,1,0:T(8,128)}, f32[9,32,256]{2,1,0:T(8,128)}, u32[]{:S(2)}, u32[]{:S(2)}) collective-permute-start(f32[9,32,256]{2,1,0:T(8,128)} %copy.23), channel_id=1, source_target_pairs={{0,1},{1,2},{2,3},{3,4},{4,5},{5,6},{6,7},{7,8},{8,9},{9,10},{10,1... | collective-permute-start | bytes 884744 | tf_op jit(solution)/shard_map/ppermute | solution.py:23
  25.6 6.6 %copy-start.1 = (f32[9,32,256]{1,2,0:T(8,128)}, f32[9,32,256]{1,2,0:T(8,128)S(1)}, u32[]{:S(2)}) copy-start(f32[9,32,256]{1,2,0:T(8,128)S(1)} %copy.26) | copy-start | bytes 884740
  122.4 10.0 %copy-start.9 = (s32[2]{0:T(128)S(1)}, s32[2]{0:T(128)}, u32[]{:S(2)}) copy-start(s32[2]{0:T(128)} %constant.131) | copy-start | bytes 28
  122.5 10.1 %copy-start.8 = (s32[2]{0:T(128)S(1)}, s32[2]{0:T(128)}, u32[]{:S(2)}) copy-start(s32[2]{0:T(128)} %constant.134) | copy-start | bytes 28
  122.5 10.9 %copy-start.2 = (f32[9,32,256]{1,2,0:T(8,128)S(1)}, f32[9,32,256]{1,2,0:T(8,128)}, u32[]{:S(2)}) copy-start(f32[9,32,256]{1,2,0:T(8,128)} %copy-done.1) | copy-start | bytes 884740
  122.5 490.7 %all-reduce.2.cloned.1.call-start = ((), (), s32[]{:S(2)}) async-start(), calls=%async_computation.2 | async-start | bytes 393216 | tf_op jit(solution)/shard_map/psum | solution.py:146
  134.5 207.5 %copy-start.4 = (f32[128,128]{1,0:T(8,128)S(1)}, f32[128,128]{1,0:T(8,128)}, u32[]{:S(2)}) copy-start(f32[128,128]{1,0:T(8,128)} %get-tuple-element.103) | copy-start | bytes 196612
  134.6 207.5 %copy-start.5 = (f32[128,128]{1,0:T(8,128)S(1)}, f32[128,128]{1,0:T(8,128)}, u32[]{:S(2)}) copy-start(f32[128,128]{1,0:T(8,128)} %get-tuple-element.105) | copy-start | bytes 196612
  134.6 207.5 %copy-start.6 = (f32[128,128]{1,0:T(8,128)S(1)}, f32[128,128]{1,0:T(8,128)}, u32[]{:S(2)}) copy-start(f32[128,128]{1,0:T(8,128)} %get-tuple-element.106) | copy-start | bytes 196612
  613.9 20.9 %collective-permute-start.2 = (f32[32,256]{1,0:T(8,128)S(1)}, f32[32,256]{1,0:T(8,128)S(1)}, u32[]{:S(2)}, u32[]{:S(2)}) collective-permute-start(f32[32,256]{1,0:T(8,128)S(1)} %get-tuple-element.88), channel_id=1, source_target_pairs={{0,1},{1,2},{2,3},{3,4},{4,5},{5,6},{6,7},{7,8},{8,9},{9,10},{10,1... | collective-permute-start | bytes 98312 | tf_op jit(solution)/shard_map/ppermute | solution.py:23
  632.1 7.3 %collective-permute-start.3 = (f32[32,256]{1,0:T(8,128)S(1)}, f32[32,256]{1,0:T(8,128)S(1)}, u32[]{:S(2)}, u32[]{:S(2)}) collective-permute-start(f32[32,256]{1,0:T(8,128)S(1)} %get-tuple-element.87), channel_id=1, source_target_pairs={{1,0},{2,1},{3,2},{4,3},{5,4},{6,5},{7,6},{8,7},{9,8},{10,9},{11,1... | collective-permute-start | bytes 98312 | tf_op jit(solution)/shard_map/ppermute | solution.py:25
  639.4 0.7 copy-start.3
Sparse Core Ops, SparseCore 0:
  122.6 214.7 reduce-scatter.1
  457.5 155.5 all-reduce.1
where the time goes:
time: 649 us; the launch traced here: 647 us
  waiting for transfers between devices  364 us (56%)
  other arithmetic  138 us (21%)
  local copies, waits for them, and re-layouts  95.7 us (15%)
  starting transfers between devices  27 us (4%)
  between operations  18.3 us (3%)
    reduce_scatter x1, waiting for transfers between devices, shards(): lax.psum_scatter(partial_value, 'beam', scatter_dimension=0, tiled=True)  203 us
    psum x1, waiting for transfers between devices, shards(): grad_strip = lax.psum(grad_strip, 'beam')  156 us
    unnamed x6, other arithmetic  121 us
    gather x80, local copies, waits for them, and re-layouts  70.9 us
    ppermute x2, starting transfers between devices, with_halo(): lax.ppermute(tail, axis, [(i, (i + 1) % count) for i in range(ends)])  22.4 us
  transfers between devices with their start and end apart: 6, of which 5 were waited for; matrix products, arithmetic and copies ran while one was open for 2% of the time, Pallas kernels for 0%

commit v1 on v0

v1 whole, which is shorter than its diff:
```python
import math

import jax
import jax.numpy as jnp
import numpy as np
from jax import lax
from jax.experimental import pallas as pl
from jax.experimental.pallas import tpu as pltpu
from jax.sharding import PartitionSpec as P

MARGIN = 32
SIGMA_SCALE = 1.0
LANES = 128
BAND = 8

VMEM = pltpu.MemorySpace.VMEM
SMEM = pltpu.MemorySpace.SMEM


def dft_blocks(length):
    index = np.arange(length)
    angle = (index[:, None] * index[None, :] % length) * (2.0 * math.pi / length)
    re = np.cos(angle) / math.sqrt(length)
    im = -np.sin(angle) / math.sqrt(length)
    forward = np.block([[re, im], [-im, re]]).astype(np.float32)
    parts = []
    for table in (forward, forward.T):
        high = table.astype(jnp.bfloat16)
        parts += [high, (table - high.astype(np.float32)).astype(jnp.bfloat16)]
    return np.stack(parts)


def split(value):
    high = value.astype(jnp.bfloat16)
    return high, (value - high.astype(jnp.float32)).astype(jnp.bfloat16)


def dot3(left, right):
    def dot(a, b):
        return jnp.dot(a, b, preferred_element_type=jnp.float32)

    return dot(left[0], right[0]) + (dot(left[0], right[1]) + dot(left[1], right[0]))


def pack_kernel(me_ref, tilt_ref, table_ref, waves_ref, out_ref, sem):
    planes = waves_ref.shape[0]
    copies = [
        pltpu.make_async_copy(
            waves_ref.at[plane, :, :, pl.ds(half * LANES, LANES)],
            out_ref.at[:, pl.ds((half * planes + plane) * BAND, BAND), :],
            sem.at[half * planes + plane],
        )
        for half in range(2)
        for plane in range(planes)
    ]
    for copy in copies:
        copy.start()
    sub = lax.broadcasted_iota(jnp.int32, (BAND, LANES), 0)
    lane = lax.broadcasted_iota(jnp.int32, (BAND, LANES), 1) - me_ref[0] * planes
    tile = jnp.zeros((BAND, LANES), jnp.float32)
    for beam in range(planes // 2):
        for part in range(2):
            here = lane == 2 * beam + part
            for row in range(4):
                value = table_ref[0, row, beam] if part == 0 else -table_ref[1, row, beam]
                tile = jnp.where(here & (sub == row), value, tile)
            for row in range(2):
                tile = jnp.where(here & (sub == 4 + row), tilt_ref[row, beam].astype(jnp.float32), tile)
    for peer in range(out_ref.shape[0]):
        out_ref[peer, 2 * planes * BAND :, :] = tile
    for copy in copies:
        copy.wait()


def exit_kernel(
    cols_ref, beside_cols_ref, spots_ref, beside_ref, recv_ref, potential_ref, own_ref, out_ref, shift_ref
):
    peers = recv_ref.shape[0]
    extra = recv_ref.shape[1] - BAND
    planes = extra // (2 * BAND)
    count = spots_ref.shape[0]

    table = recv_ref[0, extra:, :]
    for peer in range(1, peers):
        table = table + recv_ref[peer, extra:, :]
    lane = lax.broadcasted_iota(jnp.int32, (BAND, LANES), 1)
    swapped = jnp.where(
        lane % 2 == 0, -pltpu.roll(table, LANES - 1, 1), pltpu.roll(table, 1, 1)
    )
    tilt_row = table[4:5].astype(jnp.int32)
    tilt_col = table[5:6].astype(jnp.int32)

    def coefs(ref):
        row = ref[:, 0:1] - MARGIN
        col = ref[:, 1:2]
        pick = ref[:, 2:3]
        turns = (tilt_row * row + tilt_col * col) & (LANES - 1)
        angle = turns.astype(jnp.float32) * (2.0 * math.pi / LANES)
        u = jnp.zeros((count, LANES), jnp.float32)
        v = jnp.zeros((count, LANES), jnp.float32)
        for n in range(4):
            u = jnp.where(pick == n, table[n : n + 1], u)
            v = jnp.where(pick == n, swapped[n : n + 1], v)
        cosine = jnp.cos(angle)
        sine = jnp.sin(angle)
        return u * cosine + v * sine, v * cosine - u * sine

    weights = split(jnp.concatenate(coefs(spots_ref) + coefs(beside_ref), 0))
    local = potential_ref[...] * SIGMA_SCALE
    trans_re = jnp.cos(local)
    trans_im = jnp.sin(local)

    for half in range(2):
        lanes = slice(half * LANES, (half + 1) * LANES)
        for row in range(BAND):
            waves = jnp.concatenate(
                [
                    recv_ref[peer, pl.ds(half * planes * BAND + row, planes, stride=BAND), :]
                    for peer in range(peers)
                ],
                0,
            )
            summed = dot3(weights, split(waves))
            t_re = trans_re[row : row + 1, lanes]
            t_im = trans_im[row : row + 1, lanes]
            for side in range(2):
                w_re = summed[2 * side * count : (2 * side + 1) * count]
                w_im = summed[(2 * side + 1) * count : (2 * side + 2) * count]
                base = 2 * side * count * BAND + row
                shift_ref[half, pl.ds(base, count, stride=BAND), :] = t_re * w_re - t_im * w_im
                shift_ref[half, pl.ds(base + count * BAND, count, stride=BAND), :] = (
                    t_re * w_im + t_im * w_re
                )

    for side, (columns, target) in enumerate(((cols_ref, own_ref), (beside_cols_ref, out_ref))):
        for spot in range(count):
            at = columns[spot, 1]
            turn = (LANES - at) & (LANES - 1)
            for part in range(2):
                base = ((2 * side + part) * count + spot) * BAND
                left = pltpu.roll(shift_ref[0, base : base + BAND, :], turn, 1)
                right = pltpu.roll(shift_ref[1, base : base + BAND, :], turn, 1)
                target[spot, part * BAND : (part + 1) * BAND, :] = jnp.where(
                    lane < LANES - at, left, right
                )


def probe_kernel(me_ref, spots_ref, recv_ref, dft_ref, seen_ref, misfit_ref, out_ref, wave_ref, strip_ref, seen, sem):
    peers = recv_ref.shape[0]
    me = me_ref[0]
    fetch = pltpu.make_async_copy(seen_ref.at[me, 0], seen, sem)
    fetch.start()
    start_row = spots_ref[me, 0]
    start_col = spots_ref[me, 1]
    edge = MARGIN // BAND
    for part in range(2):
        for peer in range(peers):
            wave_ref[part, MARGIN + peer * BAND : MARGIN + (peer + 1) * BAND, :] = recv_ref[
                peer, part * BAND : (part + 1) * BAND, :
            ]
        for step in range(edge):
            for peer, at in ((peers - edge + step, step), (step, step + edge + peers)):
                wave_ref[part, at * BAND : (at + 1) * BAND, :] = recv_ref[
                    peer, (2 + part) * BAND : (3 + part) * BAND, :
                ]
    exit_re = wave_ref[0, pl.ds(start_row, LANES), :]
    exit_im = wave_ref[1, pl.ds(start_row, LANES), :]
    right = (dft_ref[0], dft_ref[1])
    left = (dft_ref[2], dft_ref[3])

    def transform(re, im, by_cols, by_rows):
        half = dot3(split(jnp.concatenate([re, im], 1)), by_cols)
        full = dot3(by_rows, split(jnp.concatenate([half[:, :LANES], half[:, LANES:]], 0)))
        return full[:LANES], full[LANES:]

    far_re, far_im = transform(exit_re, exit_im, right, left)
    fetch.wait()
    misfit = far_re * far_re + far_im * far_im - seen[...]
    misfit_ref[...] = misfit
    back_re, back_im = transform(misfit * far_re, misfit * far_im, left, right)
    piece = SIGMA_SCALE * (exit_re * back_im - exit_im * back_re)

    turned = pltpu.roll(piece, start_col & (LANES - 1), 1)
    lane = lax.broadcasted_iota(jnp.int32, (LANES, LANES), 1)
    strip_ref[...] = jnp.zeros(strip_ref.shape, jnp.float32)
    strip_ref[0, pl.ds(start_row, LANES), :] = jnp.where(lane >= start_col, turned, 0.0)
    strip_ref[1, pl.ds(start_row, LANES), :] = jnp.where(lane < start_col, turned, 0.0)
    for peer in range(peers):
        if peer < edge:
            beside = peer + edge + peers
        elif peer >= peers - edge:
            beside = peer - (peers - edge)
        else:
            beside = None
        for half in range(2):
            lanes = slice(half * LANES, (half + 1) * LANES)
            out_ref[peer, :BAND, lanes] = strip_ref[half, MARGIN + peer * BAND : MARGIN + (peer + 1) * BAND, :]
            out_ref[peer, BAND:, lanes] = (
                jnp.zeros((BAND, LANES), jnp.float32)
                if beside is None
                else strip_ref[half, beside * BAND : (beside + 1) * BAND, :]
            )


def beside_pairs(beams, tiles, outward):
    edge = MARGIN // BAND
    pairs = []
    for band in range(beams):
        step = -1 if band < edge else 1 if band >= beams - edge else 0
        for tile in range(tiles):
            if step and 0 <= tile + step < tiles:
                here, there = band * tiles + tile, band * tiles + tile + step
                pairs.append((here, there) if outward else (there, here))
    return pairs


def shards(
    scattering, potential, row_offset, col_offset, table_index, beam_tilt, coef_table, measured
):
    beam_dev, _, tile_rows, tile_cols = scattering.shape
    beams = lax.axis_size("beam")
    tiles = lax.axis_size("tile")
    planes = 2 * beam_dev
    count = row_offset.shape[0]
    length = measured.shape[-1]
    assert tile_rows == beams * BAND and tile_cols == 2 * LANES and length == LANES
    assert count == beams and beams * planes == LANES
    me = lax.axis_index("beam").reshape(1)

    spots = jnp.concatenate([row_offset, col_offset, table_index], 1)
    beside = lax.ppermute(spots, ("beam", "tile"), beside_pairs(beams, tiles, False))

    chunk = 2 * planes * BAND + BAND
    packed = pl.pallas_call(
        pack_kernel,
        name="pack",
        in_specs=[
            pl.BlockSpec(memory_space=SMEM),
            pl.BlockSpec(memory_space=SMEM),
            pl.BlockSpec(memory_space=SMEM),
            pl.BlockSpec(memory_space=pl.ANY),
        ],
        out_specs=pl.BlockSpec(memory_space=VMEM),
        out_shape=jax.ShapeDtypeStruct((beams, chunk, LANES), jnp.float32),
        scratch_shapes=[pltpu.SemaphoreType.DMA((2 * planes,))],
    )(me, beam_tilt, coef_table, scattering.reshape(planes, beams, BAND, tile_cols))
    bands = lax.all_to_all(packed, "beam", 0, 0, tiled=True)

    band_potential = lax.dynamic_slice_in_dim(potential, me[0] * BAND, BAND, 0)
    own, others = pl.pallas_call(
        exit_kernel,
        name="exit",
        in_specs=[pl.BlockSpec(memory_space=SMEM)] * 2 + [pl.BlockSpec(memory_space=VMEM)] * 4,
        out_specs=[pl.BlockSpec(memory_space=VMEM)] * 2,
        out_shape=[jax.ShapeDtypeStruct((count, 2 * BAND, LANES), jnp.float32)] * 2,
        scratch_shapes=[pltpu.VMEM((2, 4 * count * BAND, LANES), jnp.float32)],
    )(spots, beside, spots, beside, bands, band_potential)
    others = lax.ppermute(others, ("beam", "tile"), beside_pairs(beams, tiles, True))
    exits = lax.all_to_all(jnp.concatenate([own, others], 1), "beam", 0, 0, tiled=True)

    misfit, strips = pl.pallas_call(
        probe_kernel,
        name="probe",
        in_specs=[pl.BlockSpec(memory_space=SMEM)] * 2
        + [pl.BlockSpec(memory_space=VMEM)] * 2
        + [pl.BlockSpec(memory_space=pl.ANY)],
        out_specs=[pl.BlockSpec(memory_space=VMEM)] * 2,
        out_shape=[
            jax.ShapeDtypeStruct((length, length), jnp.float32),
            jax.ShapeDtypeStruct((beams, 2 * BAND, tile_cols), jnp.float32),
        ],
        scratch_shapes=[
            pltpu.VMEM((2, tile_rows + 2 * MARGIN, LANES), jnp.float32),
            pltpu.VMEM((2, tile_rows + 2 * MARGIN, LANES), jnp.float32),
            pltpu.VMEM((length, length), jnp.float32),
            pltpu.SemaphoreType.DMA,
        ],
    )(me, spots, exits, jnp.asarray(dft_blocks(length)), measured)

    summed = jnp.sum(lax.all_to_all(strips, "beam", 0, 0, tiled=True), 0)
    rims = lax.ppermute(summed[BAND:], ("beam", "tile"), beside_pairs(beams, tiles, False))
    band = summed[:BAND] + rims
    core = lax.all_to_all(
        jnp.broadcast_to(band[None], (beams, BAND, tile_cols)), "beam", 0, 0, tiled=True
    )
    return (misfit[None, None], core.reshape(tile_rows, tile_cols))


def solution(mesh):
    in_specs = (
        P("beam", None, "tile", None),
        P("tile", None),
        P(None, "tile"),
        P(None, "tile"),
        P(None, "tile"),
        P(None, "beam"),
        P(None, None, "beam"),
        P(None, "tile", None, None),
    )
    out_specs = (P("beam", "tile", None, None), P("tile", None))
    return jax.shard_map(shards, mesh=mesh, in_specs=in_specs, out_specs=out_specs, check_vma=False)
```

time: 649 us -> 118 us (0.18)
  the two profiles are of different devices: /device:TPU:27 before, /device:TPU:32 now
where the time goes in v1:
time: 118 us; the launch traced here: 117 us
  blocking collectives  48 us (41%)
  waiting for transfers between devices  36.9 us (31%)
  starting transfers between devices  18.8 us (16%)
  Pallas kernels  9.36 us (8%)
  local copies, waits for them, and re-layouts  2.39 us (2%)
    all_to_all x1, waiting for transfers between devices, shards(): bands = lax.all_to_all(packed, 'beam', 0, 0, tiled=True)  24.4 us
    all_to_all x1, blocking collectives, shards(): lax.all_to_all(jnp.concatenate([own, others], 1), 'beam', 0, 0, tiled=True)  18.5 us
    all_to_all x1, blocking collectives, shards(): summed = jnp.sum(lax.all_to_all(strips, 'beam', 0, 0, tiled=True), 0)  15.7 us
    all_to_all x1, blocking collectives, shards(): lax.all_to_all(jnp.broadcast_to(band[None], (beams, BAND, tile_cols)), 'b...  13.8 us
    all_to_all x1, starting transfers between devices, shards(): bands = lax.all_to_all(packed, 'beam', 0, 0, tiled=True)  13 us
    ppermute x1, waiting for transfers between devices, shards(): lax.ppermute(summed[BAND:], ('beam', 'tile'), beside_pairs(beams, tiles,...  5.15 us
    ppermute x1, waiting for transfers between devices, shards(): lax.ppermute(spots, ('beam', 'tile'), beside_pairs(beams, tiles, False))  4.54 us
    pallas_call x1, Pallas kernels, shards(): pl.pallas_call(probe_kernel, name='probe', in_specs=[pl.BlockSpec(memory_...  3.28 us
  transfers between devices with their start and end apart: 4, of which 4 were waited for; matrix products, arithmetic and copies ran while one was open for 1% of the time, Pallas kernels for 0%

profile of v1, /device:TPU:32, one launch (start us, length us, event | category | flops | bytes accessed | tf_op | source)
XLA Modules:
  0.0 117.2 jit_solution(16417833793652895893)
XLA Ops:
  0.6 0.0 copy-start
  0.7 3.2 %pack.1 = f32[16,136,128]{2,1,0:T(8,128)} custom-call(s32[1]{0:T(128)} %bitcast.me_ref, s32[2,4]{1,0:T(2,128)} %tilt_ref.1, f32[2,4,4]{2,1,0:T(4,128)} %table_ref.1, f32[8,16,8,256]{3,2,1,0:T(8,128)} %bitcast.4), custom_call_target="tpu_custom_call" | custom-call | tf_op jit(solution)/shard_map/pack/pallas_call | solution.py:234
  3.9 0.0 copy-start.4
  3.9 0.0 copy-start.5
  3.9 0.0 copy-start.6
  3.9 13.0 %all-to-all-start = ((f32[16,136,128]{2,1,0:T(8,128)}), f32[16,136,128]{2,1,0:T(8,128)S(1)}, u32[]{:S(2)}, u32[]{:S(2)}) async-start(f32[16,136,128]{2,1,0:T(8,128)} %pack.1), calls=%async_computation | async-start | bytes 2228224 | tf_op jit(solution)/shard_map/all_to_all | solution.py:247
  17.0 0.0 copy-done.4
  17.0 0.0 copy-done.5
  17.0 0.0 copy-done.6
  17.0 0.1 copy.17.cols_ref.spots_ref
  17.1 0.0 copy-start.2
  17.1 1.9 %collective-permute-start = (s32[16,3]{1,0:T(8,128)S(1)}, s32[16,3]{1,0:T(8,128)S(1)}, u32[]{:S(2)}, u32[]{:S(2)}) collective-permute-start(s32[16,3]{1,0:T(8,128)S(1)} %copy.17.cols_ref.spots_ref), channel_id=1, source_target_pairs={{0,1},{1,2},{2,3},{3,4},{4,5},{5,6},{6,7},{7,8},{8,9},{9,10},{10,1... | collective-permute-start | bytes 584 | tf_op jit(solution)/shard_map/ppermute | solution.py:231
  19.0 0.0 copy-done
  19.0 0.6 constant_dynamic-slice_fusion.potential_ref
  19.6 4.5 %collective-permute-done.beside_cols_ref.beside_ref = s32[16,3]{1,0:T(8,128)S(1)} collective-permute-done((s32[16,3]{1,0:T(8,128)S(1)}, s32[16,3]{1,0:T(8,128)S(1)}, u32[]{:S(2)}, u32[]{:S(2)}) %collective-permute-start) | collective-permute-done | bytes 224 | tf_op jit(solution)/shard_map/ppermute | solution.py:231
  24.2 0.0 copy-start.3
  24.2 24.4 %all-to-all-done.recv_ref = f32[16,136,128]{2,1,0:T(8,128)S(1)} async-done(((f32[16,136,128]{2,1,0:T(8,128)}), f32[16,136,128]{2,1,0:T(8,128)S(1)}, u32[]{:S(2)}, u32[]{:S(2)}) %all-to-all-start) | async-done | bytes 1114144 | tf_op jit(solution)/shard_map/all_to_all | solution.py:247
  48.6 0.0 copy-done.2
  48.6 0.0 copy-done.3
  48.6 0.0 copy-start.1
  48.6 1.0 copy-done.1
  49.6 2.8 %exit.1 = (f32[16,16,128]{2,1,0:T(8,128)}, f32[16,16,128]{2,1,0:T(8,128)}) custom-call(s32[16,3]{1,0:T(8,128)} %copy-done.2, s32[16,3]{1,0:T(8,128)} %copy-done.3, s32[16,3]{1,0:T(8,128)} %copy-done.2, s32[16,3]{1,0:T(8,128)} %copy-done.3, f32[16,136,128]{2,1,0:T(8,128)} %copy-done.1, f32[8,256]{1,0:T(8,128)} %constant_dynamic-slice_fusion.potential_ref), custom_call_target="tpu_custom_call" | custom-call | tf_op jit(solution)/shard_map/exit/pallas_call | solution.py:250
  52.4 1.9 %collective-permute-start.1 = (f32[16,16,128]{2,1,0:T(8,128)}, f32[16,16,128]{2,1,0:T(8,128)S(1)}, u32[]{:S(2)}, u32[]{:S(2)}) collective-permute-start(f32[16,16,128]{2,1,0:T(8,128)} %get-tuple-element.7), channel_id=1, source_target_pairs={{1,0},{2,1},{3,2},{4,3},{5,4},{6,5},{7,6},{8,7},{9,8},{10,9},{11,1... | collective-permute-start | bytes 393224 | tf_op jit(solution)/shard_map/ppermute | solution.py:258
  54.3 2.8 %collective-permute-done.1 = f32[16,16,128]{2,1,0:T(8,128)S(1)} collective-permute-done((f32[16,16,128]{2,1,0:T(8,128)}, f32[16,16,128]{2,1,0:T(8,128)S(1)}, u32[]{:S(2)}, u32[]{:S(2)}) %collective-permute-start.1) | collective-permute-done | bytes 131104 | tf_op jit(solution)/shard_map/ppermute | solution.py:258
  57.1 0.9 pad_maximum_fusion
  58.1 18.5 %all_to_all.20.recv_ref = f32[16,32,128]{2,1,0:T(8,128)} all-to-all(f32[16,32,128]{2,1,0:T(8,128)S(1)} %pad_maximum_fusion), channel_id=1, replica_groups=mesh['beam'=16,'tile'=32] {'beam'}, dimensions={0} | all-to-all | bytes 524288 | tf_op jit(solution)/shard_map/all_to_all | solution.py:259
  76.6 3.3 %probe.1 = (f32[128,128]{1,0:T(8,128)}, f32[16,16,256]{2,1,0:T(8,128)}) custom-call(s32[1]{0:T(128)} %bitcast.me_ref, s32[16,3]{1,0:T(8,128)} %copy-done.2, f32[16,32,128]{2,1,0:T(8,128)} %all_to_all.20.recv_ref, bf16[4,256,256]{2,1,0:T(8,128)(2,1)} %constant.16.clone.dft_ref, f32[16,1,128,128]{3,2,1,0:T(8,128)} %seen_ref.1), custom_call_target="tpu_custom_call" | custom-call | tf_op jit(solution)/shard_map/probe/pallas_call | solution.py:261
  79.9 15.7 %all_to_all.21 = f32[16,16,256]{2,1,0:T(8,128)S(1)} all-to-all(f32[16,16,256]{2,1,0:T(8,128)} %get-tuple-element.9), channel_id=1, replica_groups=mesh['beam'=16,'tile'=32] {'beam'}, dimensions={0} | all-to-all | bytes 524288 | tf_op jit(solution)/shard_map/all_to_all | solution.py:280
  95.6 1.9 %collective-permute-start.2 = (f32[8,256]{1,0:T(8,128)S(1)}, f32[8,256]{1,0:T(8,128)S(1)}, u32[]{:S(2)}, u32[]{:S(2)}) collective-permute-start(f32[8,256]{1,0:T(8,128)S(1)} %slice.9), channel_id=1, source_target_pairs={{0,1},{1,2},{2,3},{3,4},{4,5},{5,6},{6,7},{7,8},{8,9},{9,10},{10,1... | collective-permute-start | bytes 24584 | tf_op jit(solution)/shard_map/ppermute | solution.py:281
  97.5 5.2 %collective-permute-done.2 = f32[8,256]{1,0:T(8,128)S(1)} collective-permute-done((f32[8,256]{1,0:T(8,128)S(1)}, f32[8,256]{1,0:T(8,128)S(1)}, u32[]{:S(2)}, u32[]{:S(2)}) %collective-permute-start.2) | collective-permute-done | bytes 8224 | tf_op jit(solution)/shard_map/ppermute | solution.py:281
  102.7 13.8 %all_to_all.22 = f32[16,8,256]{2,1,0:T(8,128)S(1)} all-to-all(f32[16,8,256]{2,1,0:T(8,128)S(1)} %broadcast_in_dim.10), channel_id=1, replica_groups=mesh['beam'=16,'tile'=32] {'beam'}, dimensions={0} | all-to-all | bytes 262144 | tf_op jit(solution)/shard_map/all_to_all | solution.py:283
  116.5 0.7 copy.19
  (5 shorter events, 0.1 us)
Async XLA Ops:
  0.6 18.4 %copy-start = (f32[128,256]{1,0:T(8,128)S(1)}, f32[128,256]{1,0:T(8,128)}, u32[]{:S(2)}) copy-start(f32[128,256]{1,0:T(8,128)} %param.10) | copy-start | bytes 393220
  3.9 13.1 %copy-start.4 = (s32[16,1]{0,1:T(1,128)S(1)}, s32[16,1]{0,1:T(1,128)}, u32[]{:S(2)}) copy-start(s32[16,1]{0,1:T(1,128)} %param.13) | copy-start | bytes 196
  3.9 13.1 %copy-start.5 = (s32[16,1]{0,1:T(1,128)S(1)}, s32[16,1]{0,1:T(1,128)}, u32[]{:S(2)}) copy-start(s32[16,1]{0,1:T(1,128)} %param.12) | copy-start | bytes 196
  3.9 13.1 %copy-start.6 = (s32[16,1]{0,1:T(1,128)S(1)}, s32[16,1]{0,1:T(1,128)}, u32[]{:S(2)}) copy-start(s32[16,1]{0,1:T(1,128)} %param.11) | copy-start | bytes 196
  3.9 44.6 %all-to-all-start = ((f32[16,136,128]{2,1,0:T(8,128)}), f32[16,136,128]{2,1,0:T(8,128)S(1)}, u32[]{:S(2)}, u32[]{:S(2)}) async-start(f32[16,136,128]{2,1,0:T(8,128)} %pack.1), calls=%async_computation | async-start | bytes 2228224 | tf_op jit(solution)/shard_map/all_to_all | solution.py:247
  17.1 31.5 %copy-start.2 = (s32[16,3]{1,0:T(8,128)}, s32[16,3]{1,0:T(8,128)S(1)}, u32[]{:S(2)}) copy-start(s32[16,3]{1,0:T(8,128)S(1)} %copy.17.cols_ref.spots_ref) | copy-start | bytes 580
  17.1 7.1 %collective-permute-start = (s32[16,3]{1,0:T(8,128)S(1)}, s32[16,3]{1,0:T(8,128)S(1)}, u32[]{:S(2)}, u32[]{:S(2)}) collective-permute-start(s32[16,3]{1,0:T(8,128)S(1)} %copy.17.cols_ref.spots_ref), channel_id=1, source_target_pairs={{0,1},{1,2},{2,3},{3,4},{4,5},{5,6},{6,7},{7,8},{8,9},{9,10},{10,1... | collective-permute-start | bytes 584 | tf_op jit(solution)/shard_map/ppermute | solution.py:231
  24.2 24.4 %copy-start.3 = (s32[16,3]{1,0:T(8,128)}, s32[16,3]{1,0:T(8,128)S(1)}, u32[]{:S(2)}) copy-start(s32[16,3]{1,0:T(8,128)S(1)} %collective-permute-done.beside_cols_ref.beside_ref) | copy-start | bytes 580
  48.6 1.0 copy-start.1
  52.4 4.7 %collective-permute-start.1 = (f32[16,16,128]{2,1,0:T(8,128)}, f32[16,16,128]{2,1,0:T(8,128)S(1)}, u32[]{:S(2)}, u32[]{:S(2)}) collective-permute-start(f32[16,16,128]{2,1,0:T(8,128)} %get-tuple-element.7), channel_id=1, source_target_pairs={{1,0},{2,1},{3,2},{4,3},{5,4},{6,5},{7,6},{8,7},{9,8},{10,9},{11,1... | collective-permute-start | bytes 393224 | tf_op jit(solution)/shard_map/ppermute | solution.py:258
  95.6 7.1 %collective-permute-start.2 = (f32[8,256]{1,0:T(8,128)S(1)}, f32[8,256]{1,0:T(8,128)S(1)}, u32[]{:S(2)}, u32[]{:S(2)}) collective-permute-start(f32[8,256]{1,0:T(8,128)S(1)} %slice.9), channel_id=1, source_target_pairs={{0,1},{1,2},{2,3},{3,4},{4,5},{5,6},{6,7},{7,8},{8,9},{9,10},{10,1... | collective-permute-start | bytes 24584 | tf_op jit(solution)/shard_map/ppermute | solution.py:281

commit v2 on v1

v2 whole, which is shorter than its diff:
```python
import math

import jax
import jax.numpy as jnp
import numpy as np
from jax import lax
from jax.experimental import pallas as pl
from jax.experimental.pallas import tpu as pltpu
from jax.sharding import PartitionSpec as P

MARGIN = 32
SIGMA_SCALE = 1.0
LANES = 128
BAND = 8

VMEM = pltpu.MemorySpace.VMEM
SMEM = pltpu.MemorySpace.SMEM


def dft_blocks(length):
    index = np.arange(length)
    angle = (index[:, None] * index[None, :] % length) * (2.0 * math.pi / length)
    re = np.cos(angle) / math.sqrt(length)
    im = -np.sin(angle) / math.sqrt(length)
    forward = np.block([[re, im], [-im, re]]).astype(np.float32)
    parts = []
    for table in (forward, forward.T):
        high = table.astype(jnp.bfloat16)
        parts += [high, (table - high.astype(np.float32)).astype(jnp.bfloat16)]
    return np.stack(parts)


def split(value):
    high = value.astype(jnp.bfloat16)
    return high, (value - high.astype(jnp.float32)).astype(jnp.bfloat16)


def dot3(left, right):
    def dot(a, b):
        return jnp.dot(a, b, preferred_element_type=jnp.float32)

    return dot(left[0], right[0]) + (dot(left[0], right[1]) + dot(left[1], right[0]))


def pack_kernel(me_ref, tilt_ref, table_ref, waves_ref, out_ref, sem):
    planes = waves_ref.shape[0]
    copies = [
        pltpu.make_async_copy(
            waves_ref.at[plane, :, :, pl.ds(half * LANES, LANES)],
            out_ref.at[:, pl.ds((half * planes + plane) * BAND, BAND), :],
            sem.at[half * planes + plane],
        )
        for half in range(2)
        for plane in range(planes)
    ]
    for copy in copies:
        copy.start()
    sub = lax.broadcasted_iota(jnp.int32, (BAND, LANES), 0)
    lane = lax.broadcasted_iota(jnp.int32, (BAND, LANES), 1) - me_ref[0] * planes
    tile = jnp.zeros((BAND, LANES), jnp.float32)
    for beam in range(planes // 2):
        for part in range(2):
            here = lane == 2 * beam + part
            for row in range(4):
                value = table_ref[0, row, beam] if part == 0 else -table_ref[1, row, beam]
                tile = jnp.where(here & (sub == row), value, tile)
            for row in range(2):
                tile = jnp.where(here & (sub == 4 + row), tilt_ref[row, beam].astype(jnp.float32), tile)
    for peer in range(out_ref.shape[0]):
        out_ref[peer, 2 * planes * BAND :, :] = tile
    for copy in copies:
        copy.wait()


def exit_kernel(me_ref, spots_ref, beside_ref, recv_ref, potential_ref, own_ref, out_ref):
    peers = recv_ref.shape[0]
    extra = recv_ref.shape[1] - BAND
    planes = extra // (2 * BAND)
    count = spots_ref.shape[0]

    table = recv_ref[0, extra:, :]
    for peer in range(1, peers):
        table = table + recv_ref[peer, extra:, :]
    lane = lax.broadcasted_iota(jnp.int32, (BAND, LANES), 1)
    swapped = jnp.where(
        lane % 2 == 0, -pltpu.roll(table, LANES - 1, 1), pltpu.roll(table, 1, 1)
    )
    tilt_row = table[4:5].astype(jnp.int32)
    tilt_col = table[5:6].astype(jnp.int32)

    def coefs(ref):
        row = ref[:, 0:1] - MARGIN
        col = ref[:, 1:2]
        pick = ref[:, 2:3]
        turns = (tilt_row * row + tilt_col * col) & (LANES - 1)
        angle = turns.astype(jnp.float32) * (2.0 * math.pi / LANES)
        u = jnp.zeros((count, LANES), jnp.float32)
        v = jnp.zeros((count, LANES), jnp.float32)
        for n in range(4):
            u = jnp.where(pick == n, table[n : n + 1], u)
            v = jnp.where(pick == n, swapped[n : n + 1], v)
        cosine = jnp.cos(angle)
        sine = jnp.sin(angle)
        return u * cosine + v * sine, v * cosine - u * sine

    weights = split(jnp.concatenate(coefs(spots_ref) + coefs(beside_ref), 0))
    local = potential_ref[...] * SIGMA_SCALE
    trans_re = jnp.cos(local)
    trans_im = jnp.sin(local)
    wide = lax.broadcasted_iota(jnp.int32, (count, LANES), 1)

    for row in range(BAND):
        waves = jnp.concatenate(
            [
                jnp.concatenate(
                    [
                        recv_ref[peer, pl.ds(half * planes * BAND + row, planes, stride=BAND), :]
                        for peer in range(peers)
                    ],
                    0,
                )
                for half in range(2)
            ],
            1,
        )
        summed = dot3(weights, split(waves))
        slot = me_ref[0] * BAND + row
        for side, (ref, target) in enumerate(((spots_ref, own_ref), (beside_ref, out_ref))):
            left = wide >= ref[:, 1:2]
            start = ref[:, 0:1] - MARGIN
            inside = (start <= slot) & (start + LANES > slot)
            keep = inside if side == 0 else ~inside

            def cut(value):
                return jnp.where(left, value[:, :LANES], value[:, LANES:])

            w_re = cut(summed[2 * side * count : (2 * side + 1) * count])
            w_im = cut(summed[(2 * side + 1) * count : (2 * side + 2) * count])
            t_re = cut(trans_re[row : row + 1])
            t_im = cut(trans_im[row : row + 1])
            for part, value in enumerate((t_re * w_re - t_im * w_im, t_re * w_im + t_im * w_re)):
                target[pl.ds(part * BAND + row, count, stride=2 * BAND), :] = jnp.where(
                    keep, value, 0.0
                )


def probe_kernel(me_ref, recv_ref, dft_ref, seen_ref, misfit_ref, out_ref, seen, sem):
    fetch = pltpu.make_async_copy(seen_ref.at[me_ref[0], 0], seen, sem)
    fetch.start()
    exit_re = recv_ref[:, :BAND, :].reshape(LANES, LANES)
    exit_im = recv_ref[:, BAND:, :].reshape(LANES, LANES)
    right = (dft_ref[0], dft_ref[1])
    left = (dft_ref[2], dft_ref[3])

    def transform(re, im, by_cols, by_rows):
        half = dot3(split(jnp.concatenate([re, im], 1)), by_cols)
        full = dot3(by_rows, split(jnp.concatenate([half[:, :LANES], half[:, LANES:]], 0)))
        return full[:LANES], full[LANES:]

    far_re, far_im = transform(exit_re, exit_im, right, left)
    fetch.wait()
    misfit = far_re * far_re + far_im * far_im - seen[...]
    misfit_ref[...] = misfit
    back_re, back_im = transform(misfit * far_re, misfit * far_im, left, right)
    out_ref[...] = (SIGMA_SCALE * (exit_re * back_im - exit_im * back_re)).reshape(out_ref.shape)


def place_kernel(me_ref, spots_ref, recv_ref, core_ref, rim_ref):
    slot = lax.broadcasted_iota(jnp.int32, (BAND, LANES), 0) + me_ref[0] * BAND
    lane = lax.broadcasted_iota(jnp.int32, (BAND, LANES), 1)
    sums = [jnp.zeros((BAND, LANES), jnp.float32)] * 4
    for spot in range(recv_ref.shape[0]):
        start = spots_ref[spot, 0] - MARGIN
        inside = (slot >= start) & (slot < start + LANES)
        left = lane >= spots_ref[spot, 1]
        piece = recv_ref[spot]
        core = jnp.where(inside, piece, 0.0)
        rim = jnp.where(inside, 0.0, piece)
        parts = (jnp.where(left, core, 0.0), jnp.where(left, 0.0, core), jnp.where(left, rim, 0.0), jnp.where(left, 0.0, rim))
        sums = [total + part for total, part in zip(sums, parts)]
    core_ref[:, :LANES], core_ref[:, LANES:], rim_ref[:, :LANES], rim_ref[:, LANES:] = sums


def on_chip(shape):
    return pltpu.VMEM(shape, jnp.float32)


def near(value):
    return pltpu.with_memory_space_constraint(value, VMEM)


def beside_pairs(beams, tiles, outward):
    edge = MARGIN // BAND
    pairs = []
    for band in range(beams):
        step = -1 if band < edge else 1 if band >= beams - edge else 0
        for tile in range(tiles):
            if step and 0 <= tile + step < tiles:
                here, there = band * tiles + tile, band * tiles + tile + step
                pairs.append((here, there) if outward else (there, here))
    return pairs


def shards(
    scattering, potential, row_offset, col_offset, table_index, beam_tilt, coef_table, measured
):
    beam_dev, _, tile_rows, tile_cols = scattering.shape
    beams = lax.axis_size("beam")
    tiles = lax.axis_size("tile")
    planes = 2 * beam_dev
    count = row_offset.shape[0]
    length = measured.shape[-1]
    assert tile_rows == beams * BAND and tile_cols == 2 * LANES and length == LANES
    assert count == beams and beams * planes == LANES
    me = lax.axis_index("beam").reshape(1)
    smem = pl.BlockSpec(memory_space=SMEM)
    vmem = pl.BlockSpec(memory_space=VMEM)
    anywhere = pl.BlockSpec(memory_space=pl.ANY)

    spots = jnp.concatenate([row_offset, col_offset, table_index], 1)
    beside = lax.ppermute(spots, ("beam", "tile"), beside_pairs(beams, tiles, False))

    chunk = 2 * planes * BAND + BAND
    packed = pl.pallas_call(
        pack_kernel,
        name="pack",
        in_specs=[smem, smem, smem, anywhere],
        out_specs=vmem,
        out_shape=on_chip((beams, chunk, LANES)),
        scratch_shapes=[pltpu.SemaphoreType.DMA((2 * planes,))],
    )(me, beam_tilt, coef_table, scattering.reshape(planes, beams, BAND, tile_cols))
    bands = lax.all_to_all(packed, "beam", 0, 0, tiled=True)

    band_potential = lax.dynamic_slice_in_dim(potential, me[0] * BAND, BAND, 0)
    own, others = pl.pallas_call(
        exit_kernel,
        name="exit",
        in_specs=[smem] + [vmem] * 4,
        out_specs=[vmem] * 2,
        out_shape=[on_chip((count * 2 * BAND, LANES))] * 2,
    )(me, spots, beside, near(bands), band_potential)
    others = lax.ppermute(others, ("beam", "tile"), beside_pairs(beams, tiles, True))
    exits = lax.all_to_all((own + others).reshape(count, 2 * BAND, LANES), "beam", 0, 0, tiled=True)

    misfit, pieces = pl.pallas_call(
        probe_kernel,
        name="probe",
        in_specs=[smem, vmem, vmem, anywhere],
        out_specs=[vmem] * 2,
        out_shape=[
            jax.ShapeDtypeStruct((length, length), jnp.float32),
            on_chip((beams, BAND, LANES)),
        ],
        scratch_shapes=[pltpu.VMEM((length, length), jnp.float32), pltpu.SemaphoreType.DMA],
    )(me, near(exits), jnp.asarray(dft_blocks(length)), measured)
    pieces = lax.all_to_all(pieces, "beam", 0, 0, tiled=True)

    band, rims = pl.pallas_call(
        place_kernel,
        name="place",
        in_specs=[smem, smem, vmem],
        out_specs=[vmem] * 2,
        out_shape=[on_chip((BAND, tile_cols))] * 2,
    )(me, spots, near(pieces))
    band = band + lax.ppermute(rims, ("beam", "tile"), beside_pairs(beams, tiles, False))
    core = lax.all_to_all(
        jnp.broadcast_to(band[None], (beams, BAND, tile_cols)), "beam", 0, 0, tiled=True
    )
    return (misfit[None, None], core.reshape(tile_rows, tile_cols))


def solution(mesh):
    in_specs = (
        P("beam", None, "tile", None),
        P("tile", None),
        P(None, "tile"),
        P(None, "tile"),
        P(None, "tile"),
        P(None, "beam"),
        P(None, None, "beam"),
        P(None, "tile", None, None),
    )
    out_specs = (P("beam", "tile", None, None), P("tile", None))
    return jax.shard_map(shards, mesh=mesh, in_specs=in_specs, out_specs=out_specs, check_vma=False)
```

time: 118 us -> 111 us (0.941)
  blocking collectives: 48 us -> 44.4 us
  Pallas kernels: 9.36 us -> 8.04 us
    all_to_all x2, blocking collectives: 34.2 us -> 30.5 us  [the longest x1 17.4 us: shards(): lax.all_to_all((own + others).reshape(count, 2 * BAND, LANES), 'beam', 0,...]
    pallas_call x3 -> x4, Pallas kernels: 9.36 us -> 8.04 us  [the longest x1 3.25 us: shards(): pl.pallas_call(pack_kernel, name='pack', in_specs=[smem, smem, smem, anyw...]
where the time goes in v2:
time: 111 us; the launch traced here: 110 us
  blocking collectives  44.4 us (40%)
  waiting for transfers between devices  36.6 us (33%)
  starting transfers between devices  18.8 us (17%)
  Pallas kernels  8.04 us (7%)
  local copies, waits for them, and re-layouts  1.38 us (1%)
    all_to_all x1, waiting for transfers between devices, shards(): bands = lax.all_to_all(packed, 'beam', 0, 0, tiled=True)  24.4 us
    all_to_all x1, blocking collectives, shards(): lax.all_to_all((own + others).reshape(count, 2 * BAND, LANES), 'beam', 0,...  17.4 us
    all_to_all x1, blocking collectives, shards(): lax.all_to_all(jnp.broadcast_to(band[None], (beams, BAND, tile_cols)), 'b...  13.9 us
    all_to_all x1, blocking collectives, shards(): pieces = lax.all_to_all(pieces, 'beam', 0, 0, tiled=True)  13.2 us
    all_to_all x1, starting transfers between devices, shards(): bands = lax.all_to_all(packed, 'beam', 0, 0, tiled=True)  13 us
    ppermute x1, waiting for transfers between devices, shards(): lax.ppermute(rims, ('beam', 'tile'), beside_pairs(beams, tiles, False))  5.15 us
    ppermute x1, waiting for transfers between devices, shards(): lax.ppermute(spots, ('beam', 'tile'), beside_pairs(beams, tiles, False))  4.54 us
    pallas_call x1, Pallas kernels, shards(): pl.pallas_call(pack_kernel, name='pack', in_specs=[smem, smem, smem, anyw...  3.25 us
  transfers between devices with their start and end apart: 4, of which 4 were waited for; matrix products, arithmetic and copies ran while one was open for 1% of the time, Pallas kernels for 0%

profile of v2, /device:TPU:32, one launch (start us, length us, event | category | flops | bytes accessed | tf_op | source)
XLA Modules:
  0.0 110.0 jit_solution(449952724882953366)
XLA Ops:
  0.6 0.0 copy-start
  0.7 3.3 %pack.1 = f32[16,136,128]{2,1,0:T(8,128)} custom-call(s32[1]{0:T(128)} %bitcast.me_ref, s32[2,4]{1,0:T(2,128)} %tilt_ref.1, f32[2,4,4]{2,1,0:T(4,128)} %table_ref.1, f32[8,16,8,256]{3,2,1,0:T(8,128)} %bitcast.5), custom_call_target="tpu_custom_call" | custom-call | tf_op jit(solution)/shard_map/pack/pallas_call | solution.py:224
  3.9 0.0 copy-start.3
  3.9 0.0 copy-start.4
  3.9 0.0 copy-start.5
  3.9 13.0 %all-to-all-start = ((f32[16,136,128]{2,1,0:T(8,128)}), f32[16,136,128]{2,1,0:T(8,128)S(1)}, u32[]{:S(2)}, u32[]{:S(2)}) async-start(f32[16,136,128]{2,1,0:T(8,128)} %pack.1), calls=%async_computation | async-start | bytes 2228224 | tf_op jit(solution)/shard_map/all_to_all | solution.py:232
  17.0 0.0 copy-done.3
  17.0 0.0 copy-done.4
  17.0 0.0 copy-done.5
  17.0 0.1 copy.15.spots_ref
  17.1 0.0 copy-start.1
  17.1 1.9 %collective-permute-start = (s32[16,3]{1,0:T(8,128)S(1)}, s32[16,3]{1,0:T(8,128)S(1)}, u32[]{:S(2)}, u32[]{:S(2)}) collective-permute-start(s32[16,3]{1,0:T(8,128)S(1)} %copy.15.spots_ref), channel_id=1, source_target_pairs={{0,1},{1,2},{2,3},{3,4},{4,5},{5,6},{6,7},{7,8},{8,9},{9,10},{10,1... | collective-permute-start | bytes 584 | tf_op jit(solution)/shard_map/ppermute | solution.py:221
  19.0 0.0 copy-done
  19.0 0.6 constant_dynamic-slice_fusion.potential_ref
  19.6 4.5 %collective-permute-done.beside_ref = s32[16,3]{1,0:T(8,128)S(1)} collective-permute-done((s32[16,3]{1,0:T(8,128)S(1)}, s32[16,3]{1,0:T(8,128)S(1)}, u32[]{:S(2)}, u32[]{:S(2)}) %collective-permute-start) | collective-permute-done | bytes 224 | tf_op jit(solution)/shard_map/ppermute | solution.py:221
  24.2 0.0 copy-start.2
  24.2 24.4 %all-to-all-done.recv_ref = f32[16,136,128]{2,1,0:T(8,128)S(1)} async-done(((f32[16,136,128]{2,1,0:T(8,128)}), f32[16,136,128]{2,1,0:T(8,128)S(1)}, u32[]{:S(2)}, u32[]{:S(2)}) %all-to-all-start) | async-done | bytes 1114144 | tf_op jit(solution)/shard_map/all_to_all | solution.py:232
  48.6 0.0 copy-done.1
  48.6 0.0 copy-done.2
  48.6 1.4 %exit.1 = (f32[256,128]{1,0:T(8,128)S(1)}, f32[256,128]{1,0:T(8,128)S(1)}) custom-call(s32[1]{0:T(128)} %bitcast.me_ref, s32[16,3]{1,0:T(8,128)} %copy-done.1, s32[16,3]{1,0:T(8,128)} %copy-done.2, f32[16,136,128]{2,1,0:T(8,128)S(1)} %all-to-all-done.recv_ref, f32[8,256]{1,0:T(8,128)} %constant_dynamic-slice_fusion.potential_ref), custom_call_target="tpu_custom_call" | custom-call | tf_op jit(solution)/shard_map/exit/pallas_call | solution.py:235
  50.0 1.9 %collective-permute-start.1 = (f32[256,128]{1,0:T(8,128)S(1)}, f32[256,128]{1,0:T(8,128)S(1)}, u32[]{:S(2)}, u32[]{:S(2)}) collective-permute-start(f32[256,128]{1,0:T(8,128)S(1)} %get-tuple-element.9), channel_id=1, source_target_pairs={{1,0},{2,1},{3,2},{4,3},{5,4},{6,5},{7,6},{8,7},{9,8},{10,9},{11,1... | collective-permute-start | bytes 393224 | tf_op jit(solution)/shard_map/ppermute | solution.py:242
  51.9 2.5 %collective-permute-done.1 = f32[256,128]{1,0:T(8,128)S(1)} collective-permute-done((f32[256,128]{1,0:T(8,128)S(1)}, f32[256,128]{1,0:T(8,128)S(1)}, u32[]{:S(2)}, u32[]{:S(2)}) %collective-permute-start.1) | collective-permute-done | bytes 131104 | tf_op jit(solution)/shard_map/ppermute | solution.py:242
  54.4 17.4 %all_to_all.20.recv_ref = f32[16,16,128]{2,1,0:T(8,128)S(1)} all-to-all(f32[16,16,128]{2,1,0:T(8,128)S(1)} %bitcast.6), channel_id=1, replica_groups=mesh['beam'=16,'tile'=32] {'beam'}, dimensions={0} | all-to-all | bytes 262144 | tf_op jit(solution)/shard_map/all_to_all | solution.py:243
  71.8 2.5 %probe.1 = (f32[128,128]{1,0:T(8,128)}, f32[16,8,128]{2,1,0:T(8,128)S(1)}) custom-call(s32[1]{0:T(128)} %bitcast.me_ref, f32[16,16,128]{2,1,0:T(8,128)S(1)} %all_to_all.20.recv_ref, bf16[4,256,256]{2,1,0:T(8,128)(2,1)} %constant.14.clone.dft_ref, f32[16,1,128,128]{3,2,1,0:T(8,128)} %seen_ref.1), custom_call_target="tpu_custom_call" | custom-call | tf_op jit(solution)/shard_map/probe/pallas_call | solution.py:245
  74.3 13.2 %all_to_all.21.recv_ref = f32[16,8,128]{2,1,0:T(8,128)S(1)} all-to-all(f32[16,8,128]{2,1,0:T(8,128)S(1)} %get-tuple-element.11), channel_id=1, replica_groups=mesh['beam'=16,'tile'=32] {'beam'}, dimensions={0} | all-to-all | bytes 131072 | tf_op jit(solution)/shard_map/all_to_all | solution.py:256
  87.5 0.8 place.1
  88.4 1.9 %collective-permute-start.2 = (f32[8,256]{1,0:T(8,128)S(1)}, f32[8,256]{1,0:T(8,128)S(1)}, u32[]{:S(2)}, u32[]{:S(2)}) collective-permute-start(f32[8,256]{1,0:T(8,128)S(1)} %get-tuple-element.13), channel_id=1, source_target_pairs={{0,1},{1,2},{2,3},{3,4},{4,5},{5,6},{6,7},{7,8},{8,9},{9,10},{10,1... | collective-permute-start | bytes 24584 | tf_op jit(solution)/shard_map/ppermute | solution.py:265
  90.3 5.2 %collective-permute-done.2 = f32[8,256]{1,0:T(8,128)S(1)} collective-permute-done((f32[8,256]{1,0:T(8,128)S(1)}, f32[8,256]{1,0:T(8,128)S(1)}, u32[]{:S(2)}, u32[]{:S(2)}) %collective-permute-start.2) | collective-permute-done | bytes 8224 | tf_op jit(solution)/shard_map/ppermute | solution.py:265
  95.5 13.9 %all_to_all.22 = f32[16,8,256]{2,1,0:T(8,128)S(1)} all-to-all(f32[16,8,256]{2,1,0:T(8,128)S(1)} %broadcast_in_dim.10), channel_id=1, replica_groups=mesh['beam'=16,'tile'=32] {'beam'}, dimensions={0} | all-to-all | bytes 262144 | tf_op jit(solution)/shard_map/all_to_all | solution.py:266
  109.3 0.7 copy.18
  (4 shorter events, 0.0 us)
Async XLA Ops:
  0.6 18.4 %copy-start = (f32[128,256]{1,0:T(8,128)S(1)}, f32[128,256]{1,0:T(8,128)}, u32[]{:S(2)}) copy-start(f32[128,256]{1,0:T(8,128)} %param.10) | copy-start | bytes 393220
  3.9 13.1 %copy-start.3 = (s32[16,1]{0,1:T(1,128)S(1)}, s32[16,1]{0,1:T(1,128)}, u32[]{:S(2)}) copy-start(s32[16,1]{0,1:T(1,128)} %param.13) | copy-start | bytes 196
  3.9 13.1 %copy-start.4 = (s32[16,1]{0,1:T(1,128)S(1)}, s32[16,1]{0,1:T(1,128)}, u32[]{:S(2)}) copy-start(s32[16,1]{0,1:T(1,128)} %param.12) | copy-start | bytes 196
  3.9 13.1 %copy-start.5 = (s32[16,1]{0,1:T(1,128)S(1)}, s32[16,1]{0,1:T(1,128)}, u32[]{:S(2)}) copy-start(s32[16,1]{0,1:T(1,128)} %param.11) | copy-start | bytes 196
  3.9 44.6 %all-to-all-start = ((f32[16,136,128]{2,1,0:T(8,128)}), f32[16,136,128]{2,1,0:T(8,128)S(1)}, u32[]{:S(2)}, u32[]{:S(2)}) async-start(f32[16,136,128]{2,1,0:T(8,128)} %pack.1), calls=%async_computation | async-start | bytes 2228224 | tf_op jit(solution)/shard_map/all_to_all | solution.py:232
  17.1 31.5 %copy-start.1 = (s32[16,3]{1,0:T(8,128)}, s32[16,3]{1,0:T(8,128)S(1)}, u32[]{:S(2)}) copy-start(s32[16,3]{1,0:T(8,128)S(1)} %copy.15.spots_ref) | copy-start | bytes 580
  17.1 7.1 %collective-permute-start = (s32[16,3]{1,0:T(8,128)S(1)}, s32[16,3]{1,0:T(8,128)S(1)}, u32[]{:S(2)}, u32[]{:S(2)}) collective-permute-start(s32[16,3]{1,0:T(8,128)S(1)} %copy.15.spots_ref), channel_id=1, source_target_pairs={{0,1},{1,2},{2,3},{3,4},{4,5},{5,6},{6,7},{7,8},{8,9},{9,10},{10,1... | collective-permute-start | bytes 584 | tf_op jit(solution)/shard_map/ppermute | solution.py:221
  24.2 24.4 %copy-start.2 = (s32[16,3]{1,0:T(8,128)}, s32[16,3]{1,0:T(8,128)S(1)}, u32[]{:S(2)}) copy-start(s32[16,3]{1,0:T(8,128)S(1)} %collective-permute-done.beside_ref) | copy-start | bytes 580
  50.0 4.4 %collective-permute-start.1 = (f32[256,128]{1,0:T(8,128)S(1)}, f32[256,128]{1,0:T(8,128)S(1)}, u32[]{:S(2)}, u32[]{:S(2)}) collective-permute-start(f32[256,128]{1,0:T(8,128)S(1)} %get-tuple-element.9), channel_id=1, source_target_pairs={{1,0},{2,1},{3,2},{4,3},{5,4},{6,5},{7,6},{8,7},{9,8},{10,9},{11,1... | collective-permute-start | bytes 393224 | tf_op jit(solution)/shard_map/ppermute | solution.py:242
  88.4 7.1 %collective-permute-start.2 = (f32[8,256]{1,0:T(8,128)S(1)}, f32[8,256]{1,0:T(8,128)S(1)}, u32[]{:S(2)}, u32[]{:S(2)}) collective-permute-start(f32[8,256]{1,0:T(8,128)S(1)} %get-tuple-element.13), channel_id=1, source_target_pairs={{0,1},{1,2},{2,3},{3,4},{4,5},{5,6},{6,7},{7,8},{8,9},{9,10},{10,1... | collective-permute-start | bytes 24584 | tf_op jit(solution)/shard_map/ppermute | solution.py:265

commit v3 on v2

--- a/solution.py
+++ b/solution.py
@@ -12,6 +12,7 @@
 SIGMA_SCALE = 1.0
 LANES = 128
 BAND = 8
+SPAN = 2
 
 VMEM = pltpu.MemorySpace.VMEM
 SMEM = pltpu.MemorySpace.SMEM
@@ -42,19 +43,14 @@
     return dot(left[0], right[0]) + (dot(left[0], right[1]) + dot(left[1], right[0]))
 
 
-def pack_kernel(me_ref, tilt_ref, table_ref, waves_ref, out_ref, sem):
+def pack_kernel(me_ref, tilt_ref, table_ref, waves_ref, out_ref, held, extra, in_sem, out_sem, extra_sem):
     planes = waves_ref.shape[0]
-    copies = [
-        pltpu.make_async_copy(
-            waves_ref.at[plane, :, :, pl.ds(half * LANES, LANES)],
-            out_ref.at[:, pl.ds((half * planes + plane) * BAND, BAND), :],
-            sem.at[half * planes + plane],
-        )
-        for half in range(2)
+    loads = [
+        pltpu.make_async_copy(waves_ref.at[plane], held.at[plane], in_sem.at[plane])
         for plane in range(planes)
     ]
-    for copy in copies:
-        copy.start()
+    for load in loads:
+        load.start()
     sub = lax.broadcasted_iota(jnp.int32, (BAND, LANES), 0)
     lane = lax.broadcasted_iota(jnp.int32, (BAND, LANES), 1) - me_ref[0] * planes
     tile = jnp.zeros((BAND, LANES), jnp.float32)
@@ -67,9 +63,23 @@
             for row in range(2):
                 tile = jnp.where(here & (sub == 4 + row), tilt_ref[row, beam].astype(jnp.float32), tile)
     for peer in range(out_ref.shape[0]):
-        out_ref[peer, 2 * planes * BAND :, :] = tile
-    for copy in copies:
-        copy.wait()
+        extra[peer] = tile
+    stores = [
+        pltpu.make_async_copy(extra, out_ref.at[:, pl.ds(2 * planes * BAND, BAND), :], extra_sem)
+    ]
+    stores[0].start()
+    for plane in range(planes):
+        loads[plane].wait()
+        for half in range(2):
+            store = pltpu.make_async_copy(
+                held.at[plane, :, :, pl.ds(half * LANES, LANES)],
+                out_ref.at[:, pl.ds((half * planes + plane) * BAND, BAND), :],
+                out_sem.at[half * planes + plane],
+            )
+            store.start()
+            stores.append(store)
+    for store in stores:
+        store.wait()
 
 
 def exit_kernel(me_ref, spots_ref, beside_ref, recv_ref, potential_ref, own_ref, out_ref):
@@ -162,13 +172,18 @@
     misfit = far_re * far_re + far_im * far_im - seen[...]
     misfit_ref[...] = misfit
     back_re, back_im = transform(misfit * far_re, misfit * far_im, left, right)
-    out_ref[...] = (SIGMA_SCALE * (exit_re * back_im - exit_im * back_re)).reshape(out_ref.shape)
+    piece = SIGMA_SCALE * (exit_re * back_im - exit_im * back_re)
+    peers, rows, _ = out_ref.shape
+    for peer in range(peers):
+        at = peer // SPAN * rows
+        out_ref[peer] = piece[at : at + rows]
 
 
 def place_kernel(me_ref, spots_ref, recv_ref, core_ref, rim_ref):
-    slot = lax.broadcasted_iota(jnp.int32, (BAND, LANES), 0) + me_ref[0] * BAND
-    lane = lax.broadcasted_iota(jnp.int32, (BAND, LANES), 1)
-    sums = [jnp.zeros((BAND, LANES), jnp.float32)] * 4
+    shape = recv_ref.shape[1:]
+    slot = lax.broadcasted_iota(jnp.int32, shape, 0) + me_ref[0] // SPAN * shape[0]
+    lane = lax.broadcasted_iota(jnp.int32, shape, 1)
+    sums = [jnp.zeros(shape, jnp.float32)] * 4
     for spot in range(recv_ref.shape[0]):
         start = spots_ref[spot, 0] - MARGIN
         inside = (slot >= start) & (slot < start + LANES)
@@ -225,9 +240,15 @@
         pack_kernel,
         name="pack",
         in_specs=[smem, smem, smem, anywhere],
-        out_specs=vmem,
-        out_shape=on_chip((beams, chunk, LANES)),
-        scratch_shapes=[pltpu.SemaphoreType.DMA((2 * planes,))],
+        out_specs=anywhere,
+        out_shape=jax.ShapeDtypeStruct((beams, chunk, LANES), jnp.float32),
+        scratch_shapes=[
+            pltpu.VMEM((planes, beams, BAND, tile_cols), jnp.float32),
+            pltpu.VMEM((beams, BAND, LANES), jnp.float32),
+            pltpu.SemaphoreType.DMA((planes,)),
+            pltpu.SemaphoreType.DMA((2 * planes,)),
+            pltpu.SemaphoreType.DMA,
+        ],
     )(me, beam_tilt, coef_table, scattering.reshape(planes, beams, BAND, tile_cols))
     bands = lax.all_to_all(packed, "beam", 0, 0, tiled=True)
 
@@ -249,10 +270,10 @@
         out_specs=[vmem] * 2,
         out_shape=[
             jax.ShapeDtypeStruct((length, length), jnp.float32),
-            on_chip((beams, BAND, LANES)),
+            on_chip((beams, SPAN * BAND, LANES)),
         ],
         scratch_shapes=[pltpu.VMEM((length, length), jnp.float32), pltpu.SemaphoreType.DMA],
-    )(me, near(exits), jnp.asarray(dft_blocks(length)), measured)
+    )(me, near(exits), near(jnp.asarray(dft_blocks(length))), measured)
     pieces = lax.all_to_all(pieces, "beam", 0, 0, tiled=True)
 
     band, rims = pl.pallas_call(
@@ -260,11 +281,17 @@
         name="place",
         in_specs=[smem, smem, vmem],
         out_specs=[vmem] * 2,
-        out_shape=[on_chip((BAND, tile_cols))] * 2,
+        out_shape=[on_chip((SPAN * BAND, tile_cols))] * 2,
     )(me, spots, near(pieces))
     band = band + lax.ppermute(rims, ("beam", "tile"), beside_pairs(beams, tiles, False))
+    groups = [list(range(at, beams, SPAN)) for at in range(SPAN)]
     core = lax.all_to_all(
-        jnp.broadcast_to(band[None], (beams, BAND, tile_cols)), "beam", 0, 0, tiled=True
+        jnp.broadcast_to(band[None], (beams // SPAN, SPAN * BAND, tile_cols)),
+        "beam",
+        0,
+        0,
+        axis_index_groups=groups,
+        tiled=True,
     )
     return (misfit[None, None], core.reshape(tile_rows, tile_cols))
 

time: 111 us -> 108 us (0.973)
  blocking collectives: 44.4 us -> 42.7 us
  Pallas kernels: 8.04 us -> 6.92 us
    all_to_all x1, blocking collectives: 13.9 us -> 11.5 us  [shards(): lax.all_to_all(jnp.broadcast_to(band[None], (beams // SPAN, SPAN * BAND,...]
where the time goes in v3:
time: 108 us; the launch traced here: 107 us
  blocking collectives  42.7 us (40%)
  waiting for transfers between devices  36.5 us (34%)
  starting transfers between devices  18.9 us (17%)
  Pallas kernels  6.92 us (6%)
  local copies, waits for them, and re-layouts  1.4 us (1%)
    all_to_all x1, waiting for transfers between devices, shards(): bands = lax.all_to_all(packed, 'beam', 0, 0, tiled=True)  24.2 us
    all_to_all x1, blocking collectives, shards(): lax.all_to_all((own + others).reshape(count, 2 * BAND, LANES), 'beam', 0,...  17.4 us
    all_to_all x1, blocking collectives, shards(): pieces = lax.all_to_all(pieces, 'beam', 0, 0, tiled=True)  13.9 us
    all_to_all x1, starting transfers between devices, shards(): bands = lax.all_to_all(packed, 'beam', 0, 0, tiled=True)  13 us
    all_to_all x1, blocking collectives, shards(): lax.all_to_all(jnp.broadcast_to(band[None], (beams // SPAN, SPAN * BAND,...  11.5 us
    ppermute x1, waiting for transfers between devices, shards(): lax.ppermute(rims, ('beam', 'tile'), beside_pairs(beams, tiles, False))  5.24 us
    ppermute x1, waiting for transfers between devices, shards(): lax.ppermute(spots, ('beam', 'tile'), beside_pairs(beams, tiles, False))  4.54 us
    pallas_call x1, Pallas kernels, shards(): pl.pallas_call(pack_kernel, name='pack', in_specs=[smem, smem, smem, anyw...  3.1 us
  transfers between devices with their start and end apart: 4, of which 4 were waited for; matrix products, arithmetic and copies ran while one was open for 1% of the time, Pallas kernels for 0%

profile of v3, /device:TPU:32, one launch (start us, length us, event | category | flops | bytes accessed | tf_op | source)
XLA Modules:
  0.0 107.2 jit_solution(13821762991819120856)
XLA Ops:
  0.6 0.0 copy-start
  0.7 3.1 %pack.1 = f32[16,136,128]{2,1,0:T(8,128)} custom-call(s32[1]{0:T(128)} %bitcast.me_ref, s32[2,4]{1,0:T(2,128)} %tilt_ref.1, f32[2,4,4]{2,1,0:T(4,128)} %table_ref.1, f32[8,16,8,256]{3,2,1,0:T(8,128)} %bitcast.5), custom_call_target="tpu_custom_call" | custom-call | tf_op jit(solution)/shard_map/pack/pallas_call | solution.py:239
  3.8 0.0 copy-start.4
  3.8 0.0 copy-start.5
  3.8 0.0 copy-start.6
  3.8 13.0 %all-to-all-start = ((f32[16,136,128]{2,1,0:T(8,128)}), f32[16,136,128]{2,1,0:T(8,128)S(1)}, u32[]{:S(2)}, u32[]{:S(2)}) async-start(f32[16,136,128]{2,1,0:T(8,128)} %pack.1), calls=%async_computation | async-start | bytes 2228224 | tf_op jit(solution)/shard_map/all_to_all | solution.py:253
  16.8 0.0 copy-done.4
  16.8 0.0 copy-done.5
  16.8 0.0 copy-done.6
  16.9 0.0 copy-start.1
  16.9 0.1 copy.15.spots_ref
  17.0 0.0 copy-start.2
  17.0 2.0 %collective-permute-start = (s32[16,3]{1,0:T(8,128)S(1)}, s32[16,3]{1,0:T(8,128)S(1)}, u32[]{:S(2)}, u32[]{:S(2)}) collective-permute-start(s32[16,3]{1,0:T(8,128)S(1)} %copy.15.spots_ref), channel_id=1, source_target_pairs={{0,1},{1,2},{2,3},{3,4},{4,5},{5,6},{6,7},{7,8},{8,9},{9,10},{10,1... | collective-permute-start | bytes 584 | tf_op jit(solution)/shard_map/ppermute | solution.py:236
  19.0 0.0 copy-done
  19.0 0.6 constant_dynamic-slice_fusion.potential_ref
  19.6 4.5 %collective-permute-done.beside_ref = s32[16,3]{1,0:T(8,128)S(1)} collective-permute-done((s32[16,3]{1,0:T(8,128)S(1)}, s32[16,3]{1,0:T(8,128)S(1)}, u32[]{:S(2)}, u32[]{:S(2)}) %collective-permute-start) | collective-permute-done | bytes 224 | tf_op jit(solution)/shard_map/ppermute | solution.py:236
  24.2 0.0 copy-start.3
  24.2 24.2 %all-to-all-done.recv_ref = f32[16,136,128]{2,1,0:T(8,128)S(1)} async-done(((f32[16,136,128]{2,1,0:T(8,128)}), f32[16,136,128]{2,1,0:T(8,128)S(1)}, u32[]{:S(2)}, u32[]{:S(2)}) %all-to-all-start) | async-done | bytes 1114144 | tf_op jit(solution)/shard_map/all_to_all | solution.py:253
  48.4 0.0 copy-done.2
  48.4 0.0 copy-done.3
  48.4 1.4 %exit.1 = (f32[256,128]{1,0:T(8,128)S(1)}, f32[256,128]{1,0:T(8,128)S(1)}) custom-call(s32[1]{0:T(128)} %bitcast.me_ref, s32[16,3]{1,0:T(8,128)} %copy-done.2, s32[16,3]{1,0:T(8,128)} %copy-done.3, f32[16,136,128]{2,1,0:T(8,128)S(1)} %all-to-all-done.recv_ref, f32[8,256]{1,0:T(8,128)} %constant_dynamic-slice_fusion.potential_ref), custom_call_target="tpu_custom_call" | custom-call | tf_op jit(solution)/shard_map/exit/pallas_call | solution.py:256
  49.8 1.9 %collective-permute-start.1 = (f32[256,128]{1,0:T(8,128)S(1)}, f32[256,128]{1,0:T(8,128)S(1)}, u32[]{:S(2)}, u32[]{:S(2)}) collective-permute-start(f32[256,128]{1,0:T(8,128)S(1)} %get-tuple-element.9), channel_id=1, source_target_pairs={{1,0},{2,1},{3,2},{4,3},{5,4},{6,5},{7,6},{8,7},{9,8},{10,9},{11,1... | collective-permute-start | bytes 393224 | tf_op jit(solution)/shard_map/ppermute | solution.py:263
  51.8 2.5 %collective-permute-done.1 = f32[256,128]{1,0:T(8,128)S(1)} collective-permute-done((f32[256,128]{1,0:T(8,128)S(1)}, f32[256,128]{1,0:T(8,128)S(1)}, u32[]{:S(2)}, u32[]{:S(2)}) %collective-permute-start.1) | collective-permute-done | bytes 131104 | tf_op jit(solution)/shard_map/ppermute | solution.py:263
  54.3 17.4 %all_to_all.20.recv_ref = f32[16,16,128]{2,1,0:T(8,128)S(1)} all-to-all(f32[16,16,128]{2,1,0:T(8,128)S(1)} %bitcast.6), channel_id=1, replica_groups=mesh['beam'=16,'tile'=32] {'beam'}, dimensions={0} | all-to-all | bytes 262144 | tf_op jit(solution)/shard_map/all_to_all | solution.py:264
  71.6 0.0 copy-done.1
  71.6 1.5 %probe.1 = (f32[128,128]{1,0:T(8,128)}, f32[16,16,128]{2,1,0:T(8,128)S(1)}) custom-call(s32[1]{0:T(128)} %bitcast.me_ref, f32[16,16,128]{2,1,0:T(8,128)S(1)} %all_to_all.20.recv_ref, bf16[4,256,256]{2,1,0:T(8,128)(2,1)S(1)} %copy-done.1, f32[16,1,128,128]{3,2,1,0:T(8,128)} %seen_ref.1), custom_call_target="tpu_custom_call" | custom-call | tf_op jit(solution)/shard_map/probe/pallas_call | solution.py:266
  73.2 13.9 %all_to_all.21.recv_ref = f32[16,16,128]{2,1,0:T(8,128)S(1)} all-to-all(f32[16,16,128]{2,1,0:T(8,128)S(1)} %get-tuple-element.11), channel_id=1, replica_groups=mesh['beam'=16,'tile'=32] {'beam'}, dimensions={0} | all-to-all | bytes 262144 | tf_op jit(solution)/shard_map/all_to_all | solution.py:277
  87.0 0.9 place.1
  87.9 1.9 %collective-permute-start.2 = (f32[16,256]{1,0:T(8,128)S(1)}, f32[16,256]{1,0:T(8,128)S(1)}, u32[]{:S(2)}, u32[]{:S(2)}) collective-permute-start(f32[16,256]{1,0:T(8,128)S(1)} %get-tuple-element.13), channel_id=1, source_target_pairs={{0,1},{1,2},{2,3},{3,4},{4,5},{5,6},{6,7},{7,8},{8,9},{9,10},{10,1... | collective-permute-start | bytes 49160 | tf_op jit(solution)/shard_map/ppermute | solution.py:286
  89.8 5.2 %collective-permute-done.2 = f32[16,256]{1,0:T(8,128)S(1)} collective-permute-done((f32[16,256]{1,0:T(8,128)S(1)}, f32[16,256]{1,0:T(8,128)S(1)}, u32[]{:S(2)}, u32[]{:S(2)}) %collective-permute-start.2) | collective-permute-done | bytes 16416 | tf_op jit(solution)/shard_map/ppermute | solution.py:286
  95.1 11.5 %all_to_all.22 = f32[8,16,256]{2,1,0:T(8,128)S(1)} all-to-all(f32[8,16,256]{2,1,0:T(8,128)S(1)} %broadcast_in_dim.10), channel_id=1, replica_groups={{0,64,128,192,256,320,384,448},{32,96,160,224,288,352,416,480},{1,65,12..., dimensions={0} | all-to-all | bytes 262144 | tf_op jit(solution)/shard_map/all_to_all | solution.py:288
  106.6 0.7 copy.18
  (4 shorter events, 0.0 us)
Async XLA Ops:
  0.6 18.4 %copy-start = (f32[128,256]{1,0:T(8,128)S(1)}, f32[128,256]{1,0:T(8,128)}, u32[]{:S(2)}) copy-start(f32[128,256]{1,0:T(8,128)} %param.10) | copy-start | bytes 393220
  3.8 13.1 %copy-start.4 = (s32[16,1]{0,1:T(1,128)S(1)}, s32[16,1]{0,1:T(1,128)}, u32[]{:S(2)}) copy-start(s32[16,1]{0,1:T(1,128)} %param.13) | copy-start | bytes 196
  3.8 13.1 %copy-start.5 = (s32[16,1]{0,1:T(1,128)S(1)}, s32[16,1]{0,1:T(1,128)}, u32[]{:S(2)}) copy-start(s32[16,1]{0,1:T(1,128)} %param.12) | copy-start | bytes 196
  3.8 13.1 %copy-start.6 = (s32[16,1]{0,1:T(1,128)S(1)}, s32[16,1]{0,1:T(1,128)}, u32[]{:S(2)}) copy-start(s32[16,1]{0,1:T(1,128)} %param.11) | copy-start | bytes 196
  3.8 44.6 %all-to-all-start = ((f32[16,136,128]{2,1,0:T(8,128)}), f32[16,136,128]{2,1,0:T(8,128)S(1)}, u32[]{:S(2)}, u32[]{:S(2)}) async-start(f32[16,136,128]{2,1,0:T(8,128)} %pack.1), calls=%async_computation | async-start | bytes 2228224 | tf_op jit(solution)/shard_map/all_to_all | solution.py:253
  16.9 54.8 %copy-start.1 = (bf16[4,256,256]{2,1,0:T(8,128)(2,1)S(1)}, bf16[4,256,256]{2,1,0:T(8,128)(2,1)}, u32[]{:S(2)}) copy-start(bf16[4,256,256]{2,1,0:T(8,128)(2,1)} %constant.14.clone.dft_ref) | copy-start | bytes 1572868
  17.0 31.5 %copy-start.2 = (s32[16,3]{1,0:T(8,128)}, s32[16,3]{1,0:T(8,128)S(1)}, u32[]{:S(2)}) copy-start(s32[16,3]{1,0:T(8,128)S(1)} %copy.15.spots_ref) | copy-start | bytes 580
  17.0 7.2 %collective-permute-start = (s32[16,3]{1,0:T(8,128)S(1)}, s32[16,3]{1,0:T(8,128)S(1)}, u32[]{:S(2)}, u32[]{:S(2)}) collective-permute-start(s32[16,3]{1,0:T(8,128)S(1)} %copy.15.spots_ref), channel_id=1, source_target_pairs={{0,1},{1,2},{2,3},{3,4},{4,5},{5,6},{6,7},{7,8},{8,9},{9,10},{10,1... | collective-permute-start | bytes 584 | tf_op jit(solution)/shard_map/ppermute | solution.py:236
  24.2 24.3 %copy-start.3 = (s32[16,3]{1,0:T(8,128)}, s32[16,3]{1,0:T(8,128)S(1)}, u32[]{:S(2)}) copy-start(s32[16,3]{1,0:T(8,128)S(1)} %collective-permute-done.beside_ref) | copy-start | bytes 580
  49.8 4.4 %collective-permute-start.1 = (f32[256,128]{1,0:T(8,128)S(1)}, f32[256,128]{1,0:T(8,128)S(1)}, u32[]{:S(2)}, u32[]{:S(2)}) collective-permute-start(f32[256,128]{1,0:T(8,128)S(1)} %get-tuple-element.9), channel_id=1, source_target_pairs={{1,0},{2,1},{3,2},{4,3},{5,4},{6,5},{7,6},{8,7},{9,8},{10,9},{11,1... | collective-permute-start | bytes 393224 | tf_op jit(solution)/shard_map/ppermute | solution.py:263
  87.9 7.2 %collective-permute-start.2 = (f32[16,256]{1,0:T(8,128)S(1)}, f32[16,256]{1,0:T(8,128)S(1)}, u32[]{:S(2)}, u32[]{:S(2)}) collective-permute-start(f32[16,256]{1,0:T(8,128)S(1)} %get-tuple-element.13), channel_id=1, source_target_pairs={{0,1},{1,2},{2,3},{3,4},{4,5},{5,6},{6,7},{7,8},{8,9},{9,10},{10,1... | collective-permute-start | bytes 49160 | tf_op jit(solution)/shard_map/ppermute | solution.py:286

commit v4 on v3

--- a/solution.py
+++ b/solution.py
@@ -15,7 +15,6 @@
 SPAN = 2
 
 VMEM = pltpu.MemorySpace.VMEM
-SMEM = pltpu.MemorySpace.SMEM
 
 
 def dft_blocks(length):
@@ -43,16 +42,43 @@
     return dot(left[0], right[0]) + (dot(left[0], right[1]) + dot(left[1], right[0]))
 
 
-def pack_kernel(me_ref, tilt_ref, table_ref, waves_ref, out_ref, held, extra, in_sem, out_sem, extra_sem):
+def pack_kernel(
+    tilt_hbm,
+    table_hbm,
+    waves_ref,
+    potential_ref,
+    measured_ref,
+    out_ref,
+    band_ref,
+    seen_ref,
+    held,
+    extra,
+    tilt_ref,
+    table_ref,
+    in_sem,
+    out_sem,
+    small_sem,
+):
     planes = waves_ref.shape[0]
+    me = lax.axis_index("beam")
+    later = [
+        pltpu.make_async_copy(potential_ref.at[pl.ds(me * BAND, BAND)], band_ref, small_sem.at[3]),
+        pltpu.make_async_copy(measured_ref.at[me, 0], seen_ref, small_sem.at[4]),
+    ]
+    small = [
+        pltpu.make_async_copy(tilt_hbm, tilt_ref, small_sem.at[0]),
+        pltpu.make_async_copy(table_hbm, table_ref, small_sem.at[1]),
+    ]
     loads = [
         pltpu.make_async_copy(waves_ref.at[plane], held.at[plane], in_sem.at[plane])
         for plane in range(planes)
     ]
-    for load in loads:
+    for load in small + loads + later:
         load.start()
+    for load in small:
+        load.wait()
     sub = lax.broadcasted_iota(jnp.int32, (BAND, LANES), 0)
-    lane = lax.broadcasted_iota(jnp.int32, (BAND, LANES), 1) - me_ref[0] * planes
+    lane = lax.broadcasted_iota(jnp.int32, (BAND, LANES), 1) - me * planes
     tile = jnp.zeros((BAND, LANES), jnp.float32)
     for beam in range(planes // 2):
         for part in range(2):
@@ -65,7 +91,7 @@
     for peer in range(out_ref.shape[0]):
         extra[peer] = tile
     stores = [
-        pltpu.make_async_copy(extra, out_ref.at[:, pl.ds(2 * planes * BAND, BAND), :], extra_sem)
+        pltpu.make_async_copy(extra, out_ref.at[:, pl.ds(2 * planes * BAND, BAND), :], small_sem.at[2])
     ]
     stores[0].start()
     for plane in range(planes):
@@ -78,11 +104,11 @@
             )
             store.start()
             stores.append(store)
-    for store in stores:
-        store.wait()
-
-
-def exit_kernel(me_ref, spots_ref, beside_ref, recv_ref, potential_ref, own_ref, out_ref):
+    for copy in stores + later:
+        copy.wait()
+
+
+def exit_kernel(spots_ref, beside_ref, recv_ref, potential_ref, own_ref, out_ref):
     peers = recv_ref.shape[0]
     extra = recv_ref.shape[1] - BAND
     planes = extra // (2 * BAND)
@@ -134,7 +160,7 @@
             1,
         )
         summed = dot3(weights, split(waves))
-        slot = me_ref[0] * BAND + row
+        slot = lax.axis_index("beam") * BAND + row
         for side, (ref, target) in enumerate(((spots_ref, own_ref), (beside_ref, out_ref))):
             left = wide >= ref[:, 1:2]
             start = ref[:, 0:1] - MARGIN
@@ -154,9 +180,7 @@
                 )
 
 
-def probe_kernel(me_ref, recv_ref, dft_ref, seen_ref, misfit_ref, out_ref, seen, sem):
-    fetch = pltpu.make_async_copy(seen_ref.at[me_ref[0], 0], seen, sem)
-    fetch.start()
+def probe_kernel(recv_ref, dft_ref, seen_ref, misfit_ref, out_ref):
     exit_re = recv_ref[:, :BAND, :].reshape(LANES, LANES)
     exit_im = recv_ref[:, BAND:, :].reshape(LANES, LANES)
     right = (dft_ref[0], dft_ref[1])
@@ -168,8 +192,7 @@
         return full[:LANES], full[LANES:]
 
     far_re, far_im = transform(exit_re, exit_im, right, left)
-    fetch.wait()
-    misfit = far_re * far_re + far_im * far_im - seen[...]
+    misfit = far_re * far_re + far_im * far_im - seen_ref[...]
     misfit_ref[...] = misfit
     back_re, back_im = transform(misfit * far_re, misfit * far_im, left, right)
     piece = SIGMA_SCALE * (exit_re * back_im - exit_im * back_re)
@@ -179,15 +202,15 @@
         out_ref[peer] = piece[at : at + rows]
 
 
-def place_kernel(me_ref, spots_ref, recv_ref, core_ref, rim_ref):
+def place_kernel(spots_ref, recv_ref, core_ref, rim_ref):
     shape = recv_ref.shape[1:]
-    slot = lax.broadcasted_iota(jnp.int32, shape, 0) + me_ref[0] // SPAN * shape[0]
+    slot = lax.broadcasted_iota(jnp.int32, shape, 0) + lax.axis_index("beam") // SPAN * shape[0]
     lane = lax.broadcasted_iota(jnp.int32, shape, 1)
     sums = [jnp.zeros(shape, jnp.float32)] * 4
     for spot in range(recv_ref.shape[0]):
-        start = spots_ref[spot, 0] - MARGIN
+        start = spots_ref[spot : spot + 1, 0:1] - MARGIN
         inside = (slot >= start) & (slot < start + LANES)
-        left = lane >= spots_ref[spot, 1]
+        left = lane >= spots_ref[spot : spot + 1, 1:2]
         piece = recv_ref[spot]
         core = jnp.where(inside, piece, 0.0)
         rim = jnp.where(inside, 0.0, piece)
@@ -227,62 +250,65 @@
     length = measured.shape[-1]
     assert tile_rows == beams * BAND and tile_cols == 2 * LANES and length == LANES
     assert count == beams and beams * planes == LANES
-    me = lax.axis_index("beam").reshape(1)
-    smem = pl.BlockSpec(memory_space=SMEM)
     vmem = pl.BlockSpec(memory_space=VMEM)
     anywhere = pl.BlockSpec(memory_space=pl.ANY)
 
     spots = jnp.concatenate([row_offset, col_offset, table_index], 1)
-    beside = lax.ppermute(spots, ("beam", "tile"), beside_pairs(beams, tiles, False))
+    beside = near(lax.ppermute(spots, ("beam", "tile"), beside_pairs(beams, tiles, False)))
+    spots = near(spots)
 
     chunk = 2 * planes * BAND + BAND
-    packed = pl.pallas_call(
+    packed, band_potential, seen = pl.pallas_call(
         pack_kernel,
         name="pack",
-        in_specs=[smem, smem, smem, anywhere],
-        out_specs=anywhere,
-        out_shape=jax.ShapeDtypeStruct((beams, chunk, LANES), jnp.float32),
+        in_specs=[anywhere] * 5,
+        out_specs=[anywhere, vmem, vmem],
+        out_shape=[
+            jax.ShapeDtypeStruct((beams, chunk, LANES), jnp.float32),
+            on_chip((BAND, tile_cols)),
+            on_chip((length, length)),
+        ],
         scratch_shapes=[
             pltpu.VMEM((planes, beams, BAND, tile_cols), jnp.float32),
             pltpu.VMEM((beams, BAND, LANES), jnp.float32),
+            pltpu.SMEM(beam_tilt.shape, beam_tilt.dtype),
+            pltpu.SMEM(coef_table.shape, coef_table.dtype),
             pltpu.SemaphoreType.DMA((planes,)),
             pltpu.SemaphoreType.DMA((2 * planes,)),
-            pltpu.SemaphoreType.DMA,
+            pltpu.SemaphoreType.DMA((5,)),
         ],
-    )(me, beam_tilt, coef_table, scattering.reshape(planes, beams, BAND, tile_cols))
+    )(beam_tilt, coef_table, scattering.reshape(planes, beams, BAND, tile_cols), potential, measured)
     bands = lax.all_to_all(packed, "beam", 0, 0, tiled=True)
 
-    band_potential = lax.dynamic_slice_in_dim(potential, me[0] * BAND, BAND, 0)
     own, others = pl.pallas_call(
         exit_kernel,
         name="exit",
-        in_specs=[smem] + [vmem] * 4,
+        in_specs=[vmem] * 4,
         out_specs=[vmem] * 2,
         out_shape=[on_chip((count * 2 * BAND, LANES))] * 2,
-    )(me, spots, beside, near(bands), band_potential)
+    )(spots, beside, near(bands), near(band_potential))
     others = lax.ppermute(others, ("beam", "tile"), beside_pairs(beams, tiles, True))
     exits = lax.all_to_all((own + others).reshape(count, 2 * BAND, LANES), "beam", 0, 0, tiled=True)
 
     misfit, pieces = pl.pallas_call(
         probe_kernel,
         name="probe",
-        in_specs=[smem, vmem, vmem, anywhere],
+        in_specs=[vmem] * 3,
         out_specs=[vmem] * 2,
         out_shape=[
             jax.ShapeDtypeStruct((length, length), jnp.float32),
             on_chip((beams, SPAN * BAND, LANES)),
         ],
-        scratch_shapes=[pltpu.VMEM((length, length), jnp.float32), pltpu.SemaphoreType.DMA],
-    )(me, near(exits), near(jnp.asarray(dft_blocks(length))), measured)
+    )(near(exits), near(jnp.asarray(dft_blocks(length))), near(seen))
     pieces = lax.all_to_all(pieces, "beam", 0, 0, tiled=True)
 
     band, rims = pl.pallas_call(
         place_kernel,
         name="place",
-        in_specs=[smem, smem, vmem],
+        in_specs=[vmem] * 2,
         out_specs=[vmem] * 2,
         out_shape=[on_chip((SPAN * BAND, tile_cols))] * 2,
-    )(me, spots, near(pieces))
+    )(spots, near(pieces))
     band = band + lax.ppermute(rims, ("beam", "tile"), beside_pairs(beams, tiles, False))
     groups = [list(range(at, beams, SPAN)) for at in range(SPAN)]
     core = lax.all_to_all(

time: 108 us -> 105 us (0.972)
  Pallas kernels: 6.92 us -> 4.44 us
    pallas_call x4, Pallas kernels: 6.92 us -> 4.44 us  [the longest x1 2.23 us: shards(): pl.pallas_call(pack_kernel, name='pack', in_specs=[anywhere] * 5, out_spe...]
  transfers between devices with their start and end apart: 4 -> 4, of which waited for: 4 -> 4; matrix products, arithmetic and copies ran while one was open for 1% -> 0% of each run, Pallas kernels for 0% -> 0%
where the time goes in v4:
time: 105 us
  blocking collectives  42.7 us (41%)
  waiting for transfers between devices  37.1 us (35%)
  starting transfers between devices  18.9 us (18%)
  Pallas kernels  4.44 us (4%)
    all_to_all x1, waiting for transfers between devices, shards(): bands = lax.all_to_all(packed, 'beam', 0, 0, tiled=True)  24.3 us
    all_to_all x1, blocking collectives, shards(): lax.all_to_all((own + others).reshape(count, 2 * BAND, LANES), 'beam', 0,...  17.4 us
    all_to_all x1, blocking collectives, shards(): pieces = lax.all_to_all(pieces, 'beam', 0, 0, tiled=True)  13.8 us
    all_to_all x1, starting transfers between devices, shards(): bands = lax.all_to_all(packed, 'beam', 0, 0, tiled=True)  13 us
    all_to_all x1, blocking collectives, shards(): lax.all_to_all(jnp.broadcast_to(band[None], (beams // SPAN, SPAN * BAND,...  11.5 us
    ppermute x1, waiting for transfers between devices, shards(): lax.ppermute(rims, ('beam', 'tile'), beside_pairs(beams, tiles, False))  5.24 us
    ppermute x1, waiting for transfers between devices, shards(): lax.ppermute(spots, ('beam', 'tile'), beside_pairs(beams, tiles, False))  5.15 us
    ppermute x1, waiting for transfers between devices, shards(): lax.ppermute(others, ('beam', 'tile'), beside_pairs(beams, tiles, True))  2.5 us
  transfers between devices with their start and end apart: 4, of which 4 were waited for; matrix products, arithmetic and copies ran while one was open for 0% of the time, Pallas kernels for 0%

profile of v4, /device:TPU:32, one launch (start us, length us, event | category | flops | bytes accessed | tf_op | source)
XLA Modules:
  0.0 104.7 jit_solution(9390528314737294167)
XLA Ops:
  0.6 2.2 %pack.1 = (f32[16,136,128]{2,1,0:T(8,128)}, f32[8,256]{1,0:T(8,128)S(1)}, f32[128,128]{1,0:T(8,128)S(1)}) custom-call(s32[2,4]{1,0:T(2,128)} %tilt_hbm.1, f32[2,4,4]{2,1,0:T(4,128)} %table_hbm.1, f32[8,16,8,256]{3,2,1,0:T(8,128)} %bitcast.4, f32[128,256]{1,0:T(8,128)} %potential_ref.1, f32[16,1,128,128]{3,2,1,0:T(8,128)} %measured_ref.1), custom_call_target="tpu_custom_call" | custom-call | tf_op jit(solution)/shard_map/pack/pallas_call | solution.py:261
  2.9 0.0 copy-start.1
  2.9 0.0 copy-start.2
  2.9 0.0 copy-start.3
  2.9 13.0 %all-to-all-start = ((f32[16,136,128]{2,1,0:T(8,128)}), f32[16,136,128]{2,1,0:T(8,128)S(1)}, u32[]{:S(2)}, u32[]{:S(2)}) async-start(f32[16,136,128]{2,1,0:T(8,128)} %get-tuple-element.11), calls=%async_computation | async-start | bytes 2228224 | tf_op jit(solution)/shard_map/all_to_all | solution.py:281
  15.9 0.0 copy-done.1
  15.9 0.0 copy-done.2
  16.0 0.0 copy-done.3
  16.0 0.0 copy-start
  16.0 0.1 copy.15.spots_ref
  16.1 2.0 %collective-permute-start = (s32[16,3]{1,0:T(8,128)S(1)}, s32[16,3]{1,0:T(8,128)S(1)}, u32[]{:S(2)}, u32[]{:S(2)}) collective-permute-start(s32[16,3]{1,0:T(8,128)S(1)} %copy.15.spots_ref), channel_id=1, source_target_pairs={{0,1},{1,2},{2,3},{3,4},{4,5},{5,6},{6,7},{7,8},{8,9},{9,10},{10,1... | collective-permute-start | bytes 584 | tf_op jit(solution)/shard_map/ppermute | solution.py:257
  18.1 5.2 %collective-permute-done.beside_ref = s32[16,3]{1,0:T(8,128)S(1)} collective-permute-done((s32[16,3]{1,0:T(8,128)S(1)}, s32[16,3]{1,0:T(8,128)S(1)}, u32[]{:S(2)}, u32[]{:S(2)}) %collective-permute-start) | collective-permute-done | bytes 224 | tf_op jit(solution)/shard_map/ppermute | solution.py:257
  23.3 24.3 %all-to-all-done.recv_ref = f32[16,136,128]{2,1,0:T(8,128)S(1)} async-done(((f32[16,136,128]{2,1,0:T(8,128)}), f32[16,136,128]{2,1,0:T(8,128)S(1)}, u32[]{:S(2)}, u32[]{:S(2)}) %all-to-all-start) | async-done | bytes 1114144 | tf_op jit(solution)/shard_map/all_to_all | solution.py:281
  47.5 0.7 exit.1
  48.2 1.9 %collective-permute-start.1 = (f32[256,128]{1,0:T(8,128)S(1)}, f32[256,128]{1,0:T(8,128)S(1)}, u32[]{:S(2)}, u32[]{:S(2)}) collective-permute-start(f32[256,128]{1,0:T(8,128)S(1)} %get-tuple-element.14), channel_id=1, source_target_pairs={{1,0},{2,1},{3,2},{4,3},{5,4},{6,5},{7,6},{8,7},{9,8},{10,9},{11,1... | collective-permute-start | bytes 393224 | tf_op jit(solution)/shard_map/ppermute | solution.py:290
  50.1 2.5 %collective-permute-done.1 = f32[256,128]{1,0:T(8,128)S(1)} collective-permute-done((f32[256,128]{1,0:T(8,128)S(1)}, f32[256,128]{1,0:T(8,128)S(1)}, u32[]{:S(2)}, u32[]{:S(2)}) %collective-permute-start.1) | collective-permute-done | bytes 131104 | tf_op jit(solution)/shard_map/ppermute | solution.py:290
  52.7 17.4 %all_to_all.20.recv_ref = f32[16,16,128]{2,1,0:T(8,128)S(1)} all-to-all(f32[16,16,128]{2,1,0:T(8,128)S(1)} %bitcast.5), channel_id=1, replica_groups=mesh['beam'=16,'tile'=32] {'beam'}, dimensions={0} | all-to-all | bytes 262144 | tf_op jit(solution)/shard_map/all_to_all | solution.py:291
  70.0 0.0 copy-done
  70.0 1.4 %probe.1 = (f32[128,128]{1,0:T(8,128)}, f32[16,16,128]{2,1,0:T(8,128)S(1)}) custom-call(f32[16,16,128]{2,1,0:T(8,128)S(1)} %all_to_all.20.recv_ref, bf16[4,256,256]{2,1,0:T(8,128)(2,1)S(1)} %copy-done, f32[128,128]{1,0:T(8,128)S(1)} %get-tuple-element.15.seen_ref), custom_call_target="tpu_custom_call" | custom-call | tf_op jit(solution)/shard_map/probe/pallas_call | solution.py:293
  71.4 13.8 %all_to_all.21.recv_ref = f32[16,16,128]{2,1,0:T(8,128)S(1)} all-to-all(f32[16,16,128]{2,1,0:T(8,128)S(1)} %get-tuple-element.17), channel_id=1, replica_groups=mesh['beam'=16,'tile'=32] {'beam'}, dimensions={0} | all-to-all | bytes 262144 | tf_op jit(solution)/shard_map/all_to_all | solution.py:303
  85.2 0.2 place.1
  85.4 1.9 %collective-permute-start.2 = (f32[16,256]{1,0:T(8,128)S(1)}, f32[16,256]{1,0:T(8,128)S(1)}, u32[]{:S(2)}, u32[]{:S(2)}) collective-permute-start(f32[16,256]{1,0:T(8,128)S(1)} %get-tuple-element.19), channel_id=1, source_target_pairs={{0,1},{1,2},{2,3},{3,4},{4,5},{5,6},{6,7},{7,8},{8,9},{9,10},{10,1... | collective-permute-start | bytes 49160 | tf_op jit(solution)/shard_map/ppermute | solution.py:312
  87.3 5.2 %collective-permute-done.2 = f32[16,256]{1,0:T(8,128)S(1)} collective-permute-done((f32[16,256]{1,0:T(8,128)S(1)}, f32[16,256]{1,0:T(8,128)S(1)}, u32[]{:S(2)}, u32[]{:S(2)}) %collective-permute-start.2) | collective-permute-done | bytes 16416 | tf_op jit(solution)/shard_map/ppermute | solution.py:312
  92.6 11.5 %all_to_all.22 = f32[8,16,256]{2,1,0:T(8,128)S(1)} all-to-all(f32[8,16,256]{2,1,0:T(8,128)S(1)} %broadcast_in_dim.10), channel_id=1, replica_groups={{0,64,128,192,256,320,384,448},{32,96,160,224,288,352,416,480},{1,65,12..., dimensions={0} | all-to-all | bytes 262144 | tf_op jit(solution)/shard_map/all_to_all | solution.py:314
  104.1 0.7 copy.18
  (4 shorter events, 0.0 us)
Async XLA Ops:
  2.9 13.1 %copy-start.1 = (s32[16,1]{0,1:T(1,128)S(1)}, s32[16,1]{0,1:T(1,128)}, u32[]{:S(2)}) copy-start(s32[16,1]{0,1:T(1,128)} %param.13) | copy-start | bytes 196
  2.9 13.1 %copy-start.2 = (s32[16,1]{0,1:T(1,128)S(1)}, s32[16,1]{0,1:T(1,128)}, u32[]{:S(2)}) copy-start(s32[16,1]{0,1:T(1,128)} %param.12) | copy-start | bytes 196
  2.9 13.1 %copy-start.3 = (s32[16,1]{0,1:T(1,128)S(1)}, s32[16,1]{0,1:T(1,128)}, u32[]{:S(2)}) copy-start(s32[16,1]{0,1:T(1,128)} %param.11) | copy-start | bytes 196
  2.9 44.6 %all-to-all-start = ((f32[16,136,128]{2,1,0:T(8,128)}), f32[16,136,128]{2,1,0:T(8,128)S(1)}, u32[]{:S(2)}, u32[]{:S(2)}) async-start(f32[16,136,128]{2,1,0:T(8,128)} %get-tuple-element.11), calls=%async_computation | async-start | bytes 2228224 | tf_op jit(solution)/shard_map/all_to_all | solution.py:281
  16.0 54.1 %copy-start = (bf16[4,256,256]{2,1,0:T(8,128)(2,1)S(1)}, bf16[4,256,256]{2,1,0:T(8,128)(2,1)}, u32[]{:S(2)}) copy-start(bf16[4,256,256]{2,1,0:T(8,128)(2,1)} %constant.2.clone.dft_ref) | copy-start | bytes 1572868
  16.1 7.2 %collective-permute-start = (s32[16,3]{1,0:T(8,128)S(1)}, s32[16,3]{1,0:T(8,128)S(1)}, u32[]{:S(2)}, u32[]{:S(2)}) collective-permute-start(s32[16,3]{1,0:T(8,128)S(1)} %copy.15.spots_ref), channel_id=1, source_target_pairs={{0,1},{1,2},{2,3},{3,4},{4,5},{5,6},{6,7},{7,8},{8,9},{9,10},{10,1... | collective-permute-start | bytes 584 | tf_op jit(solution)/shard_map/ppermute | solution.py:257
  48.2 4.4 %collective-permute-start.1 = (f32[256,128]{1,0:T(8,128)S(1)}, f32[256,128]{1,0:T(8,128)S(1)}, u32[]{:S(2)}, u32[]{:S(2)}) collective-permute-start(f32[256,128]{1,0:T(8,128)S(1)} %get-tuple-element.14), channel_id=1, source_target_pairs={{1,0},{2,1},{3,2},{4,3},{5,4},{6,5},{7,6},{8,7},{9,8},{10,9},{11,1... | collective-permute-start | bytes 393224 | tf_op jit(solution)/shard_map/ppermute | solution.py:290
  85.4 7.2 %collective-permute-start.2 = (f32[16,256]{1,0:T(8,128)S(1)}, f32[16,256]{1,0:T(8,128)S(1)}, u32[]{:S(2)}, u32[]{:S(2)}) collective-permute-start(f32[16,256]{1,0:T(8,128)S(1)} %get-tuple-element.19), channel_id=1, source_target_pairs={{0,1},{1,2},{2,3},{3,4},{4,5},{5,6},{6,7},{7,8},{8,9},{9,10},{10,1... | collective-permute-start | bytes 49160 | tf_op jit(solution)/shard_map/ppermute | solution.py:312

commit v5 on v4

--- a/solution.py
+++ b/solution.py
@@ -13,6 +13,7 @@
 LANES = 128
 BAND = 8
 SPAN = 2
+PARTS = 3
 
 VMEM = pltpu.MemorySpace.VMEM
 
@@ -25,21 +26,30 @@
     forward = np.block([[re, im], [-im, re]]).astype(np.float32)
     parts = []
     for table in (forward, forward.T):
-        high = table.astype(jnp.bfloat16)
-        parts += [high, (table - high.astype(np.float32)).astype(jnp.bfloat16)]
+        rest = table
+        for _ in range(PARTS):
+            part = rest.astype(jnp.bfloat16)
+            rest = rest - part.astype(np.float32)
+            parts.append(part)
     return np.stack(parts)
 
 
 def split(value):
-    high = value.astype(jnp.bfloat16)
-    return high, (value - high.astype(jnp.float32)).astype(jnp.bfloat16)
-
-
-def dot3(left, right):
-    def dot(a, b):
-        return jnp.dot(a, b, preferred_element_type=jnp.float32)
-
-    return dot(left[0], right[0]) + (dot(left[0], right[1]) + dot(left[1], right[0]))
+    parts = []
+    for _ in range(PARTS):
+        part = value.astype(jnp.bfloat16)
+        value = value - part.astype(jnp.float32)
+        parts.append(part)
+    return parts
+
+
+def exact_dot(left, right):
+    total = None
+    for order in reversed(range(PARTS)):
+        for at in range(order + 1):
+            product = jnp.dot(left[at], right[order - at], preferred_element_type=jnp.float32)
+            total = product if total is None else total + product
+    return total
 
 
 def pack_kernel(
@@ -159,7 +169,7 @@
             ],
             1,
         )
-        summed = dot3(weights, split(waves))
+        summed = exact_dot(weights, split(waves))
         slot = lax.axis_index("beam") * BAND + row
         for side, (ref, target) in enumerate(((spots_ref, own_ref), (beside_ref, out_ref))):
             left = wide >= ref[:, 1:2]
@@ -183,12 +193,12 @@
 def probe_kernel(recv_ref, dft_ref, seen_ref, misfit_ref, out_ref):
     exit_re = recv_ref[:, :BAND, :].reshape(LANES, LANES)
     exit_im = recv_ref[:, BAND:, :].reshape(LANES, LANES)
-    right = (dft_ref[0], dft_ref[1])
-    left = (dft_ref[2], dft_ref[3])
+    right = [dft_ref[part] for part in range(PARTS)]
+    left = [dft_ref[PARTS + part] for part in range(PARTS)]
 
     def transform(re, im, by_cols, by_rows):
-        half = dot3(split(jnp.concatenate([re, im], 1)), by_cols)
-        full = dot3(by_rows, split(jnp.concatenate([half[:, :LANES], half[:, LANES:]], 0)))
+        half = exact_dot(split(jnp.concatenate([re, im], 1)), by_cols)
+        full = exact_dot(by_rows, split(jnp.concatenate([half[:, :LANES], half[:, LANES:]], 0)))
         return full[:LANES], full[LANES:]
 
     far_re, far_im = transform(exit_re, exit_im, right, left)

time: 105 us -> 106 us (level)
  no operation moved by 1% of the time
where the time goes in v5:
time: 106 us
  blocking collectives  42.7 us (40%)
  waiting for transfers between devices  37.1 us (35%)
  starting transfers between devices  18.9 us (18%)
  Pallas kernels  5.32 us (5%)
    all_to_all x1, waiting for transfers between devices, shards(): bands = lax.all_to_all(packed, 'beam', 0, 0, tiled=True)  24.3 us
    all_to_all x1, blocking collectives, shards(): lax.all_to_all((own + others).reshape(count, 2 * BAND, LANES), 'beam', 0,...  17.4 us
    all_to_all x1, blocking collectives, shards(): pieces = lax.all_to_all(pieces, 'beam', 0, 0, tiled=True)  13.8 us
    all_to_all x1, starting transfers between devices, shards(): bands = lax.all_to_all(packed, 'beam', 0, 0, tiled=True)  13 us
    all_to_all x1, blocking collectives, shards(): lax.all_to_all(jnp.broadcast_to(band[None], (beams // SPAN, SPAN * BAND,...  11.5 us
    ppermute x1, waiting for transfers between devices, shards(): lax.ppermute(rims, ('beam', 'tile'), beside_pairs(beams, tiles, False))  5.24 us
    ppermute x1, waiting for transfers between devices, shards(): lax.ppermute(spots, ('beam', 'tile'), beside_pairs(beams, tiles, False))  5.15 us
    ppermute x1, waiting for transfers between devices, shards(): lax.ppermute(others, ('beam', 'tile'), beside_pairs(beams, tiles, True))  2.5 us
  transfers between devices with their start and end apart: 4, of which 4 were waited for; matrix products, arithmetic and copies ran while one was open for 0% of the time, Pallas kernels for 0%

profile of v5, /device:TPU:32, one launch (start us, length us, event | category | flops | bytes accessed | tf_op | source)
XLA Modules:
  0.0 105.6 jit_solution(10006281139992807612)
XLA Ops:
  0.6 2.2 %pack.1 = (f32[16,136,128]{2,1,0:T(8,128)}, f32[8,256]{1,0:T(8,128)S(1)}, f32[128,128]{1,0:T(8,128)S(1)}) custom-call(s32[2,4]{1,0:T(2,128)} %tilt_hbm.1, f32[2,4,4]{2,1,0:T(4,128)} %table_hbm.1, f32[8,16,8,256]{3,2,1,0:T(8,128)} %bitcast.4, f32[128,256]{1,0:T(8,128)} %potential_ref.1, f32[16,1,128,128]{3,2,1,0:T(8,128)} %measured_ref.1), custom_call_target="tpu_custom_call" | custom-call | tf_op jit(solution)/shard_map/pack/pallas_call | solution.py:271
  2.9 0.0 copy-start.1
  2.9 0.0 copy-start.2
  2.9 0.0 copy-start.3
  2.9 13.0 %all-to-all-start = ((f32[16,136,128]{2,1,0:T(8,128)}), f32[16,136,128]{2,1,0:T(8,128)S(1)}, u32[]{:S(2)}, u32[]{:S(2)}) async-start(f32[16,136,128]{2,1,0:T(8,128)} %get-tuple-element.11), calls=%async_computation | async-start | bytes 2228224 | tf_op jit(solution)/shard_map/all_to_all | solution.py:291
  15.9 0.0 copy-done.1
  15.9 0.0 copy-done.2
  16.0 0.0 copy-done.3
  16.0 0.0 copy-start
  16.0 0.1 copy.15.spots_ref
  16.1 2.0 %collective-permute-start = (s32[16,3]{1,0:T(8,128)S(1)}, s32[16,3]{1,0:T(8,128)S(1)}, u32[]{:S(2)}, u32[]{:S(2)}) collective-permute-start(s32[16,3]{1,0:T(8,128)S(1)} %copy.15.spots_ref), channel_id=1, source_target_pairs={{0,1},{1,2},{2,3},{3,4},{4,5},{5,6},{6,7},{7,8},{8,9},{9,10},{10,1... | collective-permute-start | bytes 584 | tf_op jit(solution)/shard_map/ppermute | solution.py:267
  18.1 5.2 %collective-permute-done.beside_ref = s32[16,3]{1,0:T(8,128)S(1)} collective-permute-done((s32[16,3]{1,0:T(8,128)S(1)}, s32[16,3]{1,0:T(8,128)S(1)}, u32[]{:S(2)}, u32[]{:S(2)}) %collective-permute-start) | collective-permute-done | bytes 224 | tf_op jit(solution)/shard_map/ppermute | solution.py:267
  23.3 24.3 %all-to-all-done.recv_ref = f32[16,136,128]{2,1,0:T(8,128)S(1)} async-done(((f32[16,136,128]{2,1,0:T(8,128)}), f32[16,136,128]{2,1,0:T(8,128)S(1)}, u32[]{:S(2)}, u32[]{:S(2)}) %all-to-all-start) | async-done | bytes 1114144 | tf_op jit(solution)/shard_map/all_to_all | solution.py:291
  47.5 0.9 exit.1
  48.4 1.9 %collective-permute-start.1 = (f32[256,128]{1,0:T(8,128)S(1)}, f32[256,128]{1,0:T(8,128)S(1)}, u32[]{:S(2)}, u32[]{:S(2)}) collective-permute-start(f32[256,128]{1,0:T(8,128)S(1)} %get-tuple-element.14), channel_id=1, source_target_pairs={{1,0},{2,1},{3,2},{4,3},{5,4},{6,5},{7,6},{8,7},{9,8},{10,9},{11,1... | collective-permute-start | bytes 393224 | tf_op jit(solution)/shard_map/ppermute | solution.py:300
  50.3 2.5 %collective-permute-done.1 = f32[256,128]{1,0:T(8,128)S(1)} collective-permute-done((f32[256,128]{1,0:T(8,128)S(1)}, f32[256,128]{1,0:T(8,128)S(1)}, u32[]{:S(2)}, u32[]{:S(2)}) %collective-permute-start.1) | collective-permute-done | bytes 131104 | tf_op jit(solution)/shard_map/ppermute | solution.py:300
  52.9 17.4 %all_to_all.20.recv_ref = f32[16,16,128]{2,1,0:T(8,128)S(1)} all-to-all(f32[16,16,128]{2,1,0:T(8,128)S(1)} %bitcast.5), channel_id=1, replica_groups=mesh['beam'=16,'tile'=32] {'beam'}, dimensions={0} | all-to-all | bytes 262144 | tf_op jit(solution)/shard_map/all_to_all | solution.py:301
  70.2 0.0 copy-done
  70.2 2.1 %probe.1 = (f32[128,128]{1,0:T(8,128)}, f32[16,16,128]{2,1,0:T(8,128)S(1)}) custom-call(f32[16,16,128]{2,1,0:T(8,128)S(1)} %all_to_all.20.recv_ref, bf16[6,256,256]{2,1,0:T(8,128)(2,1)S(1)} %copy-done, f32[128,128]{1,0:T(8,128)S(1)} %get-tuple-element.15.seen_ref), custom_call_target="tpu_custom_call" | custom-call | tf_op jit(solution)/shard_map/probe/pallas_call | solution.py:303
  72.3 13.8 %all_to_all.21.recv_ref = f32[16,16,128]{2,1,0:T(8,128)S(1)} all-to-all(f32[16,16,128]{2,1,0:T(8,128)S(1)} %get-tuple-element.17), channel_id=1, replica_groups=mesh['beam'=16,'tile'=32] {'beam'}, dimensions={0} | all-to-all | bytes 262144 | tf_op jit(solution)/shard_map/all_to_all | solution.py:313
  86.1 0.2 place.1
  86.3 1.9 %collective-permute-start.2 = (f32[16,256]{1,0:T(8,128)S(1)}, f32[16,256]{1,0:T(8,128)S(1)}, u32[]{:S(2)}, u32[]{:S(2)}) collective-permute-start(f32[16,256]{1,0:T(8,128)S(1)} %get-tuple-element.19), channel_id=1, source_target_pairs={{0,1},{1,2},{2,3},{3,4},{4,5},{5,6},{6,7},{7,8},{8,9},{9,10},{10,1... | collective-permute-start | bytes 49160 | tf_op jit(solution)/shard_map/ppermute | solution.py:322
  88.2 5.2 %collective-permute-done.2 = f32[16,256]{1,0:T(8,128)S(1)} collective-permute-done((f32[16,256]{1,0:T(8,128)S(1)}, f32[16,256]{1,0:T(8,128)S(1)}, u32[]{:S(2)}, u32[]{:S(2)}) %collective-permute-start.2) | collective-permute-done | bytes 16416 | tf_op jit(solution)/shard_map/ppermute | solution.py:322
  93.5 11.5 %all_to_all.22 = f32[8,16,256]{2,1,0:T(8,128)S(1)} all-to-all(f32[8,16,256]{2,1,0:T(8,128)S(1)} %broadcast_in_dim.10), channel_id=1, replica_groups={{0,64,128,192,256,320,384,448},{32,96,160,224,288,352,416,480},{1,65,12..., dimensions={0} | all-to-all | bytes 262144 | tf_op jit(solution)/shard_map/all_to_all | solution.py:324
  104.9 0.7 copy.18
  (4 shorter events, 0.0 us)
Async XLA Ops:
  2.9 13.1 %copy-start.1 = (s32[16,1]{0,1:T(1,128)S(1)}, s32[16,1]{0,1:T(1,128)}, u32[]{:S(2)}) copy-start(s32[16,1]{0,1:T(1,128)} %param.13) | copy-start | bytes 196
  2.9 13.1 %copy-start.2 = (s32[16,1]{0,1:T(1,128)S(1)}, s32[16,1]{0,1:T(1,128)}, u32[]{:S(2)}) copy-start(s32[16,1]{0,1:T(1,128)} %param.12) | copy-start | bytes 196
  2.9 13.1 %copy-start.3 = (s32[16,1]{0,1:T(1,128)S(1)}, s32[16,1]{0,1:T(1,128)}, u32[]{:S(2)}) copy-start(s32[16,1]{0,1:T(1,128)} %param.11) | copy-start | bytes 196
  2.9 44.6 %all-to-all-start = ((f32[16,136,128]{2,1,0:T(8,128)}), f32[16,136,128]{2,1,0:T(8,128)S(1)}, u32[]{:S(2)}, u32[]{:S(2)}) async-start(f32[16,136,128]{2,1,0:T(8,128)} %get-tuple-element.11), calls=%async_computation | async-start | bytes 2228224 | tf_op jit(solution)/shard_map/all_to_all | solution.py:291
  16.0 54.2 %copy-start = (bf16[6,256,256]{2,1,0:T(8,128)(2,1)S(1)}, bf16[6,256,256]{2,1,0:T(8,128)(2,1)}, u32[]{:S(2)}) copy-start(bf16[6,256,256]{2,1,0:T(8,128)(2,1)} %constant.2.clone.dft_ref) | copy-start | bytes 2359300
  16.1 7.2 %collective-permute-start = (s32[16,3]{1,0:T(8,128)S(1)}, s32[16,3]{1,0:T(8,128)S(1)}, u32[]{:S(2)}, u32[]{:S(2)}) collective-permute-start(s32[16,3]{1,0:T(8,128)S(1)} %copy.15.spots_ref), channel_id=1, source_target_pairs={{0,1},{1,2},{2,3},{3,4},{4,5},{5,6},{6,7},{7,8},{8,9},{9,10},{10,1... | collective-permute-start | bytes 584 | tf_op jit(solution)/shard_map/ppermute | solution.py:267
  48.4 4.4 %collective-permute-start.1 = (f32[256,128]{1,0:T(8,128)S(1)}, f32[256,128]{1,0:T(8,128)S(1)}, u32[]{:S(2)}, u32[]{:S(2)}) collective-permute-start(f32[256,128]{1,0:T(8,128)S(1)} %get-tuple-element.14), channel_id=1, source_target_pairs={{1,0},{2,1},{3,2},{4,3},{5,4},{6,5},{7,6},{8,7},{9,8},{10,9},{11,1... | collective-permute-start | bytes 393224 | tf_op jit(solution)/shard_map/ppermute | solution.py:300
  86.3 7.2 %collective-permute-start.2 = (f32[16,256]{1,0:T(8,128)S(1)}, f32[16,256]{1,0:T(8,128)S(1)}, u32[]{:S(2)}, u32[]{:S(2)}) collective-permute-start(f32[16,256]{1,0:T(8,128)S(1)} %get-tuple-element.19), channel_id=1, source_target_pairs={{0,1},{1,2},{2,3},{3,4},{4,5},{5,6},{6,7},{7,8},{8,9},{9,10},{10,1... | collective-permute-start | bytes 49160 | tf_op jit(solution)/shard_map/ppermute | solution.py:322

commit v6 on v4

--- a/solution.py
+++ b/solution.py
@@ -1,3 +1,4 @@
+import functools
 import math
 
 import jax
@@ -36,10 +37,9 @@
 
 
 def dot3(left, right):
-    def dot(a, b):
-        return jnp.dot(a, b, preferred_element_type=jnp.float32)
-
-    return dot(left[0], right[0]) + (dot(left[0], right[1]) + dot(left[1], right[0]))
+    lefts = jnp.concatenate([left[0], left[1], left[0]], 1)
+    rights = jnp.concatenate([right[0], right[0], right[1]], 0)
+    return jnp.dot(lefts, rights, preferred_element_type=jnp.float32)
 
 
 def pack_kernel(
@@ -108,7 +108,7 @@
         copy.wait()
 
 
-def exit_kernel(spots_ref, beside_ref, recv_ref, potential_ref, own_ref, out_ref):
+def exit_kernel(own, spots_ref, recv_ref, potential_ref, out_ref):
     peers = recv_ref.shape[0]
     extra = recv_ref.shape[1] - BAND
     planes = extra // (2 * BAND)
@@ -139,7 +139,7 @@
         sine = jnp.sin(angle)
         return u * cosine + v * sine, v * cosine - u * sine
 
-    weights = split(jnp.concatenate(coefs(spots_ref) + coefs(beside_ref), 0))
+    weights = split(jnp.concatenate(coefs(spots_ref), 0))
     local = potential_ref[...] * SIGMA_SCALE
     trans_re = jnp.cos(local)
     trans_im = jnp.sin(local)
@@ -161,23 +161,20 @@
         )
         summed = dot3(weights, split(waves))
         slot = lax.axis_index("beam") * BAND + row
-        for side, (ref, target) in enumerate(((spots_ref, own_ref), (beside_ref, out_ref))):
-            left = wide >= ref[:, 1:2]
-            start = ref[:, 0:1] - MARGIN
-            inside = (start <= slot) & (start + LANES > slot)
-            keep = inside if side == 0 else ~inside
-
-            def cut(value):
-                return jnp.where(left, value[:, :LANES], value[:, LANES:])
-
-            w_re = cut(summed[2 * side * count : (2 * side + 1) * count])
-            w_im = cut(summed[(2 * side + 1) * count : (2 * side + 2) * count])
-            t_re = cut(trans_re[row : row + 1])
-            t_im = cut(trans_im[row : row + 1])
-            for part, value in enumerate((t_re * w_re - t_im * w_im, t_re * w_im + t_im * w_re)):
-                target[pl.ds(part * BAND + row, count, stride=2 * BAND), :] = jnp.where(
-                    keep, value, 0.0
-                )
+        left = wide >= spots_ref[:, 1:2]
+        start = spots_ref[:, 0:1] - MARGIN
+        inside = (start <= slot) & (start + LANES > slot)
+        keep = inside if own else ~inside
+
+        def cut(value):
+            return jnp.where(left, value[:, :LANES], value[:, LANES:])
+
+        w_re = cut(summed[:count])
+        w_im = cut(summed[count:])
+        t_re = cut(trans_re[row : row + 1])
+        t_im = cut(trans_im[row : row + 1])
+        for part, value in enumerate((t_re * w_re - t_im * w_im, t_re * w_im + t_im * w_re)):
+            out_ref[pl.ds(part * BAND + row, count, stride=2 * BAND), :] = jnp.where(keep, value, 0.0)
 
 
 def probe_kernel(recv_ref, dft_ref, seen_ref, misfit_ref, out_ref):
@@ -280,14 +277,22 @@
     )(beam_tilt, coef_table, scattering.reshape(planes, beams, BAND, tile_cols), potential, measured)
     bands = lax.all_to_all(packed, "beam", 0, 0, tiled=True)
 
-    own, others = pl.pallas_call(
-        exit_kernel,
-        name="exit",
-        in_specs=[vmem] * 4,
-        out_specs=[vmem] * 2,
-        out_shape=[on_chip((count * 2 * BAND, LANES))] * 2,
-    )(spots, beside, near(bands), near(band_potential))
-    others = lax.ppermute(others, ("beam", "tile"), beside_pairs(beams, tiles, True))
+    bands = near(bands)
+    band_potential = near(band_potential)
+
+    def exits_of(positions, own):
+        return pl.pallas_call(
+            functools.partial(exit_kernel, own),
+            name="exit_own" if own else "exit_beside",
+            in_specs=[vmem] * 3,
+            out_specs=vmem,
+            out_shape=on_chip((count * 2 * BAND, LANES)),
+        )(positions, bands, band_potential)
+
+    others = lax.ppermute(
+        exits_of(beside, False), ("beam", "tile"), beside_pairs(beams, tiles, True)
+    )
+    own = exits_of(spots, True)
     exits = lax.all_to_all((own + others).reshape(count, 2 * BAND, LANES), "beam", 0, 0, tiled=True)
 
     misfit, pieces = pl.pallas_call(

time: 105 us -> 105 us (level)
  transfers between devices with their start and end apart: 4 -> 4, of which waited for: 4 -> 4; matrix products, arithmetic and copies ran while one was open for 0% -> 0% of each run, Pallas kernels for 0% -> 1%
where the time goes in v6:
time: 105 us
  blocking collectives  42.7 us (41%)
  waiting for transfers between devices  36.7 us (35%)
  starting transfers between devices  18.9 us (18%)
  Pallas kernels  4.97 us (5%)
    all_to_all x1, waiting for transfers between devices, shards(): bands = lax.all_to_all(packed, 'beam', 0, 0, tiled=True)  24.4 us
    all_to_all x1, blocking collectives, shards(): lax.all_to_all((own + others).reshape(count, 2 * BAND, LANES), 'beam', 0,...  17.4 us
    all_to_all x1, blocking collectives, shards(): pieces = lax.all_to_all(pieces, 'beam', 0, 0, tiled=True)  13.8 us
    all_to_all x1, starting transfers between devices, shards(): bands = lax.all_to_all(packed, 'beam', 0, 0, tiled=True)  13 us
    all_to_all x1, blocking collectives, shards(): lax.all_to_all(jnp.broadcast_to(band[None], (beams // SPAN, SPAN * BAND,...  11.5 us
    ppermute x1, waiting for transfers between devices, shards(): lax.ppermute(rims, ('beam', 'tile'), beside_pairs(beams, tiles, False))  5.24 us
    ppermute x1, waiting for transfers between devices, shards(): lax.ppermute(spots, ('beam', 'tile'), beside_pairs(beams, tiles, False))  5.15 us
    pallas_call x1, Pallas kernels, shards(): pl.pallas_call(pack_kernel, name='pack', in_specs=[anywhere] * 5, out_spe...  2.26 us
  transfers between devices with their start and end apart: 4, of which 4 were waited for; matrix products, arithmetic and copies ran while one was open for 0% of the time, Pallas kernels for 1%

profile of v6, /device:TPU:32, one launch (start us, length us, event | category | flops | bytes accessed | tf_op | source)
XLA Modules:
  0.0 104.8 jit_solution(6212650253902485315)
XLA Ops:
  0.6 2.3 %pack.1 = (f32[16,136,128]{2,1,0:T(8,128)}, f32[8,256]{1,0:T(8,128)S(1)}, f32[128,128]{1,0:T(8,128)S(1)}) custom-call(s32[2,4]{1,0:T(2,128)} %tilt_hbm.1, f32[2,4,4]{2,1,0:T(4,128)} %table_hbm.1, f32[8,16,8,256]{3,2,1,0:T(8,128)} %bitcast.4, f32[128,256]{1,0:T(8,128)} %potential_ref.1, f32[16,1,128,128]{3,2,1,0:T(8,128)} %measured_ref.1), custom_call_target="tpu_custom_call" | custom-call | tf_op jit(solution)/shard_map/pack/pallas_call | solution.py:258
  2.9 0.0 copy-start.1
  2.9 0.0 copy-start.2
  2.9 0.0 copy-start.3
  2.9 13.0 %all-to-all-start = ((f32[16,136,128]{2,1,0:T(8,128)}), f32[16,136,128]{2,1,0:T(8,128)S(1)}, u32[]{:S(2)}, u32[]{:S(2)}) async-start(f32[16,136,128]{2,1,0:T(8,128)} %get-tuple-element.9), calls=%async_computation | async-start | bytes 2228224 | tf_op jit(solution)/shard_map/all_to_all | solution.py:278
  16.0 0.0 copy-done.1
  16.0 0.0 copy-done.2
  16.0 0.0 copy-done.3
  16.0 0.1 copy.14.spots_ref
  16.1 1.9 %collective-permute-start = (s32[16,3]{1,0:T(8,128)S(1)}, s32[16,3]{1,0:T(8,128)S(1)}, u32[]{:S(2)}, u32[]{:S(2)}) collective-permute-start(s32[16,3]{1,0:T(8,128)S(1)} %copy.14.spots_ref), channel_id=1, source_target_pairs={{0,1},{1,2},{2,3},{3,4},{4,5},{5,6},{6,7},{7,8},{8,9},{9,10},{10,1... | collective-permute-start | bytes 584 | tf_op jit(solution)/shard_map/ppermute | solution.py:254
  18.0 5.2 %collective-permute-done.spots_ref = s32[16,3]{1,0:T(8,128)S(1)} collective-permute-done((s32[16,3]{1,0:T(8,128)S(1)}, s32[16,3]{1,0:T(8,128)S(1)}, u32[]{:S(2)}, u32[]{:S(2)}) %collective-permute-start) | collective-permute-done | bytes 224 | tf_op jit(solution)/shard_map/ppermute | solution.py:254
  23.2 24.4 %all-to-all-done.recv_ref = f32[16,136,128]{2,1,0:T(8,128)S(1)} async-done(((f32[16,136,128]{2,1,0:T(8,128)}), f32[16,136,128]{2,1,0:T(8,128)S(1)}, u32[]{:S(2)}, u32[]{:S(2)}) %all-to-all-start) | async-done | bytes 1114144 | tf_op jit(solution)/shard_map/all_to_all | solution.py:278
  47.6 0.6 exit_beside.1
  48.2 0.0 copy-start
  48.2 2.1 %collective-permute-start.1 = (f32[256,128]{1,0:T(8,128)S(1)}, f32[256,128]{1,0:T(8,128)S(1)}, u32[]{:S(2)}, u32[]{:S(2)}) collective-permute-start(f32[256,128]{1,0:T(8,128)S(1)} %exit_beside.1), channel_id=1, source_target_pairs={{1,0},{2,1},{3,2},{4,3},{5,4},{6,5},{7,6},{8,7},{9,8},{10,9},{11,1... | collective-permute-start | bytes 393224 | tf_op jit(solution)/shard_map/ppermute | solution.py:292
  50.2 0.6 exit_own.1
  50.8 1.9 %collective-permute-done.1 = f32[256,128]{1,0:T(8,128)S(1)} collective-permute-done((f32[256,128]{1,0:T(8,128)S(1)}, f32[256,128]{1,0:T(8,128)S(1)}, u32[]{:S(2)}, u32[]{:S(2)}) %collective-permute-start.1) | collective-permute-done | bytes 131104 | tf_op jit(solution)/shard_map/ppermute | solution.py:292
  52.7 17.4 %all_to_all.20.recv_ref = f32[16,16,128]{2,1,0:T(8,128)S(1)} all-to-all(f32[16,16,128]{2,1,0:T(8,128)S(1)} %bitcast.5), channel_id=1, replica_groups=mesh['beam'=16,'tile'=32] {'beam'}, dimensions={0} | all-to-all | bytes 262144 | tf_op jit(solution)/shard_map/all_to_all | solution.py:296
  70.1 0.0 copy-done
  70.1 1.4 %probe.1 = (f32[128,128]{1,0:T(8,128)}, f32[16,16,128]{2,1,0:T(8,128)S(1)}) custom-call(f32[16,16,128]{2,1,0:T(8,128)S(1)} %all_to_all.20.recv_ref, bf16[4,256,256]{2,1,0:T(8,128)(2,1)S(1)} %copy-done, f32[128,128]{1,0:T(8,128)S(1)} %get-tuple-element.11.seen_ref), custom_call_target="tpu_custom_call" | custom-call | tf_op jit(solution)/shard_map/probe/pallas_call | solution.py:298
  71.5 13.8 %all_to_all.21.recv_ref = f32[16,16,128]{2,1,0:T(8,128)S(1)} all-to-all(f32[16,16,128]{2,1,0:T(8,128)S(1)} %get-tuple-element.13), channel_id=1, replica_groups=mesh['beam'=16,'tile'=32] {'beam'}, dimensions={0} | all-to-all | bytes 262144 | tf_op jit(solution)/shard_map/all_to_all | solution.py:308
  85.3 0.2 place.1
  85.5 1.9 %collective-permute-start.2 = (f32[16,256]{1,0:T(8,128)S(1)}, f32[16,256]{1,0:T(8,128)S(1)}, u32[]{:S(2)}, u32[]{:S(2)}) collective-permute-start(f32[16,256]{1,0:T(8,128)S(1)} %get-tuple-element.15), channel_id=1, source_target_pairs={{0,1},{1,2},{2,3},{3,4},{4,5},{5,6},{6,7},{7,8},{8,9},{9,10},{10,1... | collective-permute-start | bytes 49160 | tf_op jit(solution)/shard_map/ppermute | solution.py:317
  87.4 5.2 %collective-permute-done.2 = f32[16,256]{1,0:T(8,128)S(1)} collective-permute-done((f32[16,256]{1,0:T(8,128)S(1)}, f32[16,256]{1,0:T(8,128)S(1)}, u32[]{:S(2)}, u32[]{:S(2)}) %collective-permute-start.2) | collective-permute-done | bytes 16416 | tf_op jit(solution)/shard_map/ppermute | solution.py:317
  92.7 11.5 %all_to_all.22 = f32[8,16,256]{2,1,0:T(8,128)S(1)} all-to-all(f32[8,16,256]{2,1,0:T(8,128)S(1)} %broadcast_in_dim.10), channel_id=1, replica_groups={{0,64,128,192,256,320,384,448},{32,96,160,224,288,352,416,480},{1,65,12..., dimensions={0} | all-to-all | bytes 262144 | tf_op jit(solution)/shard_map/all_to_all | solution.py:319
  104.1 0.7 copy.18
  (4 shorter events, 0.0 us)
Async XLA Ops:
  2.9 13.1 %copy-start.1 = (s32[16,1]{0,1:T(1,128)S(1)}, s32[16,1]{0,1:T(1,128)}, u32[]{:S(2)}) copy-start(s32[16,1]{0,1:T(1,128)} %param.13) | copy-start | bytes 196
  2.9 13.1 %copy-start.2 = (s32[16,1]{0,1:T(1,128)S(1)}, s32[16,1]{0,1:T(1,128)}, u32[]{:S(2)}) copy-start(s32[16,1]{0,1:T(1,128)} %param.12) | copy-start | bytes 196
  2.9 13.1 %copy-start.3 = (s32[16,1]{0,1:T(1,128)S(1)}, s32[16,1]{0,1:T(1,128)}, u32[]{:S(2)}) copy-start(s32[16,1]{0,1:T(1,128)} %param.11) | copy-start | bytes 196
  2.9 44.6 %all-to-all-start = ((f32[16,136,128]{2,1,0:T(8,128)}), f32[16,136,128]{2,1,0:T(8,128)S(1)}, u32[]{:S(2)}, u32[]{:S(2)}) async-start(f32[16,136,128]{2,1,0:T(8,128)} %get-tuple-element.9), calls=%async_computation | async-start | bytes 2228224 | tf_op jit(solution)/shard_map/all_to_all | solution.py:278
  16.1 7.1 %collective-permute-start = (s32[16,3]{1,0:T(8,128)S(1)}, s32[16,3]{1,0:T(8,128)S(1)}, u32[]{:S(2)}, u32[]{:S(2)}) collective-permute-start(s32[16,3]{1,0:T(8,128)S(1)} %copy.14.spots_ref), channel_id=1, source_target_pairs={{0,1},{1,2},{2,3},{3,4},{4,5},{5,6},{6,7},{7,8},{8,9},{9,10},{10,1... | collective-permute-start | bytes 584 | tf_op jit(solution)/shard_map/ppermute | solution.py:254
  48.2 21.9 %copy-start = (bf16[4,256,256]{2,1,0:T(8,128)(2,1)S(1)}, bf16[4,256,256]{2,1,0:T(8,128)(2,1)}, u32[]{:S(2)}) copy-start(bf16[4,256,256]{2,1,0:T(8,128)(2,1)} %constant.2.clone.dft_ref) | copy-start | bytes 1572868
  48.2 4.6 %collective-permute-start.1 = (f32[256,128]{1,0:T(8,128)S(1)}, f32[256,128]{1,0:T(8,128)S(1)}, u32[]{:S(2)}, u32[]{:S(2)}) collective-permute-start(f32[256,128]{1,0:T(8,128)S(1)} %exit_beside.1), channel_id=1, source_target_pairs={{1,0},{2,1},{3,2},{4,3},{5,4},{6,5},{7,6},{8,7},{9,8},{10,9},{11,1... | collective-permute-start | bytes 393224 | tf_op jit(solution)/shard_map/ppermute | solution.py:292
  85.5 7.2 %collective-permute-start.2 = (f32[16,256]{1,0:T(8,128)S(1)}, f32[16,256]{1,0:T(8,128)S(1)}, u32[]{:S(2)}, u32[]{:S(2)}) collective-permute-start(f32[16,256]{1,0:T(8,128)S(1)} %get-tuple-element.15), channel_id=1, source_target_pairs={{0,1},{1,2},{2,3},{3,4},{4,5},{5,6},{6,7},{7,8},{8,9},{9,10},{10,1... | collective-permute-start | bytes 49160 | tf_op jit(solution)/shard_map/ppermute | solution.py:317
